TPU v7x, 256 devices: a whole 4x4x8 slice. The times are simulated.
256 devices in a mesh: sec: 2 (over core), row: 16 (over y_hi, z), col: 8 (over y_lo, x).
Axes of the slice: x: 4, y: 4 (y_hi: 2, y_lo: 2; y = y_hi * 2 + y_lo), z: 8, core: 2. Of those that a mesh axis runs over, the one named last changes fastest.
Arguments:
- grid_terms: float32 [768, 1536, 128], P(('row', 'col'), 'sec'), may hold values from -6 to 6
- pair_orders: int32 [256], replicated, may hold values from 0 to 255, each once
- legendre: bfloat16 [256, 513, 768], P(('sec', 'row', 'col')), may hold values from -0.21875 to 0.21875
- state: bfloat16 [256, 513, 256], P(('sec', 'row', 'col')), may hold values from -6 to 6
- kappa: float32 [128], replicated, may hold values from 0.05 to 5
- right_op: bfloat16 [128, 128], replicated, may hold values from -0.5 to 0.5
- left_op: bfloat16 [128, 128], replicated, may hold values from -0.5 to 0.5
Outputs:
- evolved: float32 [768, 1536, 128], P(('row', 'col'), 'sec')
- new_state: bfloat16 [256, 513, 256], P(('sec', 'row', 'col'))
Inputs may be any that keep to these rules, and one draw needn't show every extreme that they name: pair_orders is a permutation: each order below 256 is the lower order of exactly one pair.
All inputs are finite; a program needn't handle non-finite values.
Results may differ from a plain program's by a relative error of at most 0.0085.
Values may be sent and summed in bfloat16 or wider, within the bound.
A program may use at most 64 MiB of HBM per device.

v0:
```python
import math

import jax
import jax.numpy as jnp
from jax import lax
from jax.sharding import PartitionSpec as P

time_step = 0.5
filter_strength = 36.0
filter_power = 36.0


def slot_orders_of(pair_orders):
    order_total = 2 * pair_orders.shape[0]
    return jnp.stack([pair_orders, order_total - 1 - pair_orders], axis=1).reshape(order_total)


def fourier_table(orders, phi_start, phi_count, longitudes):
    longitude = phi_start + lax.iota(jnp.int32, phi_count)
    phase_turns = longitude[:, None] * orders[None, :] % longitudes
    phase_angle = phase_turns.astype(jnp.float32) * (2.0 * math.pi / longitudes)
    norm_scale = 1.0 / math.sqrt(longitudes)
    return jnp.stack(
        [jnp.cos(phase_angle) * norm_scale, -jnp.sin(phase_angle) * norm_scale], axis=-1
    )


def on_device(grid_terms, pair_orders, legendre, state, kappa, right_op, left_op):
    lat_rows, phi_count, radial = grid_terms.shape
    pairs_here = legendre.shape[0]
    degrees = legendre.shape[1] - 1
    latitudes = legendre.shape[2]
    sections = lax.axis_size("sec")
    longitudes = phi_count * sections
    columns = 2 * radial
    section_slots = degrees // sections
    orders = slot_orders_of(pair_orders)
    sec_index = lax.axis_index("sec")
    highest = lax.Precision.HIGHEST
    phi_start = sec_index * phi_count
    sub_orders = orders
    phase_table = fourier_table(sub_orders, phi_start, phi_count, longitudes)
    term = jnp.einsum(
        "tpr,psc->stcr",
        grid_terms,
        phase_table,
        precision=highest,
        preferred_element_type=jnp.float32,
    )
    spectral = lax.psum_scatter(
        term.reshape(section_slots * lax.axis_size("sec"), lat_rows, columns),
        "sec",
        scatter_dimension=0,
        tiled=True,
    ).astype(jnp.bfloat16)
    device = lax.axis_index(("sec", "row", "col"))
    local_orders = lax.dynamic_slice_in_dim(pair_orders, device * pairs_here, pairs_here)
    row_index = lax.iota(jnp.int32, degrees + 1)
    leading = row_index[None, :] < (degrees - local_orders)[:, None]
    degree = jnp.where(leading, local_orders[:, None] + row_index[None, :], row_index[None, :] - 1)
    received = lax.all_to_all(spectral, ("row", "col"), split_axis=0, concat_axis=1, tiled=True)
    item_count = received.shape[2]
    paired = received.reshape(pairs_here, 2, latitudes, item_count)
    both_orders = jnp.einsum("pit,potx->piox", legendre, paired, preferred_element_type=jnp.float32)
    coefficient = jnp.where(leading[:, :, None], both_orders[:, :, 0], both_orders[:, :, 1])
    right_side = (state.astype(jnp.float32) + time_step * coefficient).astype(jnp.bfloat16)
    right_side = right_side.reshape(pairs_here, degrees + 1, 2, radial)
    eigen_part = jnp.einsum(
        "picr,rk->pick", right_side, right_op, preferred_element_type=jnp.float32
    )
    radial_mode = lax.iota(jnp.float32, radial) / radial
    damping = jnp.exp(-filter_strength * radial_mode**filter_power)
    degree_wide = degree.astype(jnp.float32)
    degree_term = degree_wide * (degree_wide + 1.0) / (degrees * degrees)
    factor = damping[None, None, :] / (1.0 + kappa[None, None, :] + degree_term[:, :, None])
    scaled = (eigen_part * factor[:, :, None, :]).astype(jnp.bfloat16)
    new_state = jnp.einsum("pick,kr->picr", scaled, left_op, preferred_element_type=jnp.float32)
    new_state = new_state.astype(jnp.bfloat16).reshape(pairs_here, degrees + 1, columns)
    zero_rows = jnp.zeros_like(new_state)
    split_state = jnp.stack(
        [
            jnp.where(leading[:, :, None], new_state, zero_rows),
            jnp.where(leading[:, :, None], zero_rows, new_state),
        ],
        axis=1,
    )
    synthesis_wide = jnp.einsum(
        "pit,poix->potx", legendre, split_state, preferred_element_type=jnp.float32
    )
    synthesis = synthesis_wide.astype(jnp.bfloat16).reshape(2 * pairs_here, latitudes, columns)
    returned = lax.all_to_all(synthesis, ("row", "col"), split_axis=1, concat_axis=0, tiled=True)
    sub_orders = lax.dynamic_slice_in_dim(orders, sec_index * section_slots, section_slots)
    phase_table = fourier_table(sub_orders, 0, longitudes, longitudes)
    values = returned.astype(jnp.float32).reshape(section_slots, lat_rows, 2, radial)
    partial_value = jnp.einsum(
        "stcr,psc->tpr", values, phase_table, precision=highest, preferred_element_type=jnp.float32
    )
    evolved = lax.psum_scatter(
        partial_value.astype(jnp.bfloat16), "sec", scatter_dimension=1, tiled=True
    ).astype(jnp.float32)
    return (evolved, new_state)


def solution(mesh):
    return jax.shard_map(
        on_device,
        mesh=mesh,
        in_specs=(
            P(("row", "col"), "sec", None),
            P(),
            P(("sec", "row", "col"), None, None),
            P(("sec", "row", "col"), None, None),
            P(),
            P(),
            P(),
        ),
        out_specs=(P(("row", "col"), "sec", None), P(("sec", "row", "col"), None, None)),
        check_vma=False,
    )
```

profile of v0, /device:TPU:1, one launch (start us, length us, event | category | flops | bytes accessed | tf_op | source)
XLA Modules:
  0.0 165.5 jit_solution(12810259262066612721)
XLA Ops:
  7.2 0.0 copy-start
  7.2 0.0 reduce-scatter.3.cloned.1.call-start
  7.2 0.8 broadcast_subtract_fusion
  8.1 0.7 pad_add_fusion
  8.8 0.1 copy.34
  8.9 0.1 reshape.494
  9.0 6.5 %cosine_multiply_fusion = (f32[768,512,1]{1,0,2:T(8,128)S(1)}, f32[768,512,1]{1,0,2:T(8,128)S(1)}) fusion(s32[512]{0:T(512)S(1)} %reshape.494, s32[768]{0:T(1024)S(1)} %iota_add_fusion), kind=kLoop, calls=%fused_computation.18 | loop fusion | flops 4718592 | bytes 3150848 | tf_op jit(solution)/shard_map/mul | solution.py:24
  15.5 0.0 copy-done
  15.6 8.4 %fusion.7 = f32[512,6,2,128]{0,3,1,2:T(8,128)S(1)} fusion(f32[6,768,128]{2,1,0:T(8,128)S(1)} %copy-done, f32[768,512,1]{1,0,2:T(8,128)S(1)} %get-tuple-element.5, f32[768,512,1]{1,0,2:T(8,128)S(1)} %get-tuple-element.4), kind=kOutput, calls=%fused_computation.12 | convolution fusion | flops 7248543744 | bytes 8650752 | tf_op jit(solution)/shard_map/tpr,psc->stcr/dot_general | solution.py:43
  24.0 2.0 %copy.36 = f32[512,6,2,128]{0,3,2,1:T(8,128)} copy(f32[512,6,2,128]{0,3,1,2:T(8,128)S(1)} %fusion.7) | data formatting | bytes 6291456 | tf_op jit(solution)/shard_map/tpr,psc->stcr/transpose | solution.py:43
  25.9 0.0 reduce-scatter.3.cloned.1.call-update
  26.0 20.4 %reduce-scatter.3.cloned.1.call-done = f32[256,6,256]{0,2,1:T(8,128)} async-done(((f32[512,6,256]{0,2,1:T(8,128)}), f32[256,6,256]{0,2,1:T(8,128)}) %reduce-scatter.3.cloned.1.call-update) | async-done | bytes 1572880 | tf_op jit(solution)/shard_map/reduce_scatter | solution.py:50
  46.4 1.5 convert_element_type.76
  47.9 0.0 copy-start.6
  47.9 0.0 copy-start.7
  47.9 1.7 %copy.37 = bf16[256,6,256]{2,1,0:T(8,128)(2,1)} copy(bf16[256,6,256]{0,2,1:T(8,128)(2,1)S(1)} %convert_element_type.76) | data formatting | bytes 1572864 | tf_op jit(solution)/shard_map/convert_element_type | solution.py:55
  49.7 14.1 %all-to-all-start = ((bf16[256,6,256]{2,1,0:T(8,128)(2,1)}), bf16[256,6,256]{2,1,0:T(8,128)(2,1)S(1)}, u32[]{:S(2)}, u32[]{:S(2)}) async-start(bf16[256,6,256]{2,1,0:T(8,128)(2,1)} %copy.37), calls=%async_computation.1 | async-start | bytes 2097152 | tf_op jit(solution)/shard_map/all_to_all | solution.py:61
  63.7 0.0 copy-done.6
  63.7 0.6 dynamic_slice.7
  65.0 0.7 fusion.38
  65.6 0.0 copy-done.7
  65.7 0.9 add_divide_fusion
  66.5 27.5 %all-to-all-done = bf16[256,6,256]{2,1,0:T(8,128)(2,1)S(1)} async-done(((bf16[256,6,256]{2,1,0:T(8,128)(2,1)}), bf16[256,6,256]{2,1,0:T(8,128)(2,1)S(1)}, u32[]{:S(2)}, u32[]{:S(2)}) %all-to-all-start) | async-done | bytes 786464 | tf_op jit(solution)/shard_map/all_to_all | solution.py:61
  94.1 0.0 copy-start.2
  94.1 0.6 copy.51
  94.7 0.0 copy-start.3
  94.7 0.5 copy-done.2
  95.2 0.6 convolution_bitcast_fusion
  95.8 0.0 copy-done.3
  95.8 0.0 copy-start.1
  95.8 0.0 copy-start.4
  95.8 0.0 copy-start.5
  95.8 0.2 fusion.29
  96.0 0.3 reshape.498
  96.3 0.5 copy-done.1
  96.8 0.0 copy-done.4
  96.8 0.0 copy-done.5
  96.8 0.5 convolution_convert_fusion.1
  97.3 0.2 copy.52
  97.5 0.4 reshape.499
  98.0 0.1 broadcast_select_fusion.1
  98.1 2.0 %fusion.20 = bf16[2,768,256]{1,2,0:T(8,128)(2,1)S(1)} fusion(bf16[1,513,768]{2,1,0:T(8,128)(2,1)} %param.9, bf16[1,1,513,256]{3,2,1,0:T(8,128)(2,1)S(1)} %get-tuple-element.3, bf16[1,1,513,256]{3,2,1,0:T(8,128)(2,1)S(1)} %get-tuple-element.2), kind=kOutput, calls=%fused_computation.31 | convolution fusion | flops 404095488 | bytes 2099712 | tf_op jit(solution)/shard_map/pit,poix->potx/dot_general | solution.py:87
  100.1 1.8 %copy.43 = bf16[2,768,256]{2,0,1:T(2,128)(2,1)} copy(bf16[2,768,256]{1,2,0:T(8,128)(2,1)S(1)} %fusion.20) | data formatting | bytes 1572864 | tf_op jit(solution)/shard_map/reshape | solution.py:90
  101.9 6.2 %all-to-all-start.1 = ((bf16[2,768,256]{2,0,1:T(2,128)(2,1)}), bf16[2,768,256]{2,0,1:T(2,128)(2,1)S(1)}, u32[]{:S(2)}, u32[]{:S(2)}) async-start(bf16[2,768,256]{2,0,1:T(2,128)(2,1)} %copy.43), calls=%async_computation.2 | async-start | bytes 1572864 | tf_op jit(solution)/shard_map/all_to_all | solution.py:91
  108.1 0.3 reduce-scatter.5.cloned.1.call-start
  108.4 0.1 dynamic_slice.6
  108.4 7.5 %cosine_multiply_fusion.1 = (f32[1536,256,1]{1,0,2:T(8,128)}, f32[1536,256,1]{1,0,2:T(8,128)}) fusion(s32[256]{0:T(256)S(1)} %dynamic_slice.6), kind=kLoop, calls=%fused_computation.23 | loop fusion | flops 4718592 | bytes 3146752 | tf_op jit(solution)/shard_map/mul | solution.py:24
  115.9 14.5 %all-to-all-done.1 = bf16[2,768,256]{2,0,1:T(2,128)(2,1)S(1)} async-done(((bf16[2,768,256]{2,0,1:T(2,128)(2,1)}), bf16[2,768,256]{2,0,1:T(2,128)(2,1)S(1)}, u32[]{:S(2)}, u32[]{:S(2)}) %all-to-all-start.1) | async-done | bytes 786464 | tf_op jit(solution)/shard_map/all_to_all | solution.py:91
  130.4 1.4 copy.44
  131.8 2.9 %reshape.502 = bf16[256,6,2,128]{3,2,0,1:T(2,128)(2,1)S(1)} reshape(bf16[128,2,6,256]{3,1,0,2:T(2,128)(2,1)} %copy.44) | data formatting | bytes 1572864 | tf_op jit(solution)/shard_map/reshape | solution.py:94
  134.7 8.2 %fusion.5 = bf16[6,1536,128]{2,1,0:T(8,128)(2,1)} fusion(f32[1536,256,1]{1,0,2:T(8,128)} %get-tuple-element.7, f32[1536,256,1]{1,0,2:T(8,128)} %get-tuple-element.6, bf16[256,6,2,128]{3,2,0,1:T(2,128)(2,1)S(1)} %reshape.502), kind=kOutput, calls=%fused_computation.8 | convolution fusion | flops 7249723392 | bytes 6291456 | tf_op jit(solution)/shard_map/stcr,psc->tpr/dot_general | solution.py:95
  142.9 0.0 reduce-scatter.5.cloned.1.call-update
  142.9 1.1 reshape.503
  144.1 11.7 %reduce-scatter.5.cloned.1.call-done = bf16[6,768,128]{2,1,0:T(8,128)(2,1)} async-done(((bf16[6,1536,128]{2,1,0:T(8,128)(2,1)}), bf16[6,768,128]{2,1,0:T(8,128)(2,1)}) %reduce-scatter.5.cloned.1.call-update) | async-done | bytes 1179664 | tf_op jit(solution)/shard_map/reduce_scatter | solution.py:98
  155.8 2.8 %convert_element_type.86 = f32[6,768,128]{2,1,0:T(8,128)} convert(bf16[6,768,128]{2,1,0:T(8,128)(2,1)} %reduce-scatter.5.cloned.1.call-done) | non-fusion elementwise | flops 589824 | bytes 3538944 | tf_op jit(solution)/shard_map/convert_element_type | solution.py:100
  (3 shorter events, 0.0 us)
Async XLA Ops:
  7.2 8.4 %copy-start = (f32[6,768,128]{2,1,0:T(8,128)S(1)}, f32[6,768,128]{2,1,0:T(8,128)}, u32[]{:S(2)}) copy-start(f32[6,768,128]{2,1,0:T(8,128)} %param.7) | copy-start | bytes 7077892
  7.2 39.2 %reduce-scatter.3.cloned.1.call-start = ((), (), s32[]{:S(2)}) async-start(), calls=%async_computation.4 | async-start | bytes 4718592 | tf_op jit(solution)/shard_map/reduce_scatter | solution.py:50
  47.9 15.8 %copy-start.6 = (s32[256]{0:T(256)S(1)}, s32[256]{0:T(256)}, u32[]{:S(2)}) copy-start(s32[256]{0:T(256)} %param.8) | copy-start | bytes 3076
  47.9 17.8 %copy-start.7 = (f32[128]{0:T(128)S(1)}, f32[128]{0:T(128)}, u32[]{:S(2)}) copy-start(f32[128]{0:T(128)} %param.11) | copy-start | bytes 1540
  49.7 44.4 %all-to-all-start = ((bf16[256,6,256]{2,1,0:T(8,128)(2,1)}), bf16[256,6,256]{2,1,0:T(8,128)(2,1)S(1)}, u32[]{:S(2)}, u32[]{:S(2)}) async-start(bf16[256,6,256]{2,1,0:T(8,128)(2,1)} %copy.37), calls=%async_computation.1 | async-start | bytes 2097152 | tf_op jit(solution)/shard_map/all_to_all | solution.py:61
  94.1 1.1 copy-start.2
  94.7 1.1 copy-start.3
  95.8 1.0 copy-start.1
  95.8 0.9 copy-start.4
  95.8 0.9 copy-start.5
  101.9 28.5 %all-to-all-start.1 = ((bf16[2,768,256]{2,0,1:T(2,128)(2,1)}), bf16[2,768,256]{2,0,1:T(2,128)(2,1)S(1)}, u32[]{:S(2)}, u32[]{:S(2)}) async-start(bf16[2,768,256]{2,0,1:T(2,128)(2,1)} %copy.43), calls=%async_computation.2 | async-start | bytes 1572864 | tf_op jit(solution)/shard_map/all_to_all | solution.py:91
  108.1 47.7 %reduce-scatter.5.cloned.1.call-start = ((), (), s32[]{:S(2)}) async-start(), calls=%async_computation.5 | async-start | bytes 3538944 | tf_op jit(solution)/shard_map/reduce_scatter | solution.py:98
Sparse Core Ops, SparseCore 0:
  26.1 20.2 reduce-scatter.2
  143.0 12.7 reduce-scatter.4
where the time goes:
time: 166 us; the launch traced here: 165 us
  waiting for transfers between devices  74.2 us (45%)
  other arithmetic  21.6 us (13%)
  starting transfers between devices  20.5 us (12%)
  matrix products  19.7 us (12%)
  between operations  14.9 us (9%)
  local copies, waits for them, and re-layouts  14.5 us (9%)
    all_to_all x1, waiting for transfers between devices, on_device(): lax.all_to_all(spectral, ('row', 'col'), split_axis=0, concat_axis=1, til...  27.5 us
    reduce_scatter x1, waiting for transfers between devices, on_device(): lax.psum_scatter(term.reshape(section_slots * lax.axis_size('sec'), lat_r...  20.4 us
    all_to_all x1, waiting for transfers between devices, on_device(): lax.all_to_all(synthesis, ('row', 'col'), split_axis=1, concat_axis=0, ti...  14.5 us
    all_to_all x1, starting transfers between devices, on_device(): lax.all_to_all(spectral, ('row', 'col'), split_axis=0, concat_axis=1, til...  14.1 us
    mul x2, other arithmetic, fourier_table(): jnp.cos(phase_angle) * norm_scale  14 us
    reduce_scatter x1, waiting for transfers between devices, on_device(): lax.psum_scatter(partial_value.astype(jnp.bfloat16), 'sec', scatter_dimen...  11.7 us
    dot_general x1, matrix products, on_device(): jnp.einsum('tpr,psc->stcr', grid_terms, phase_table, precision=highest, p...  8.4 us
    dot_general x1, matrix products, on_device(): jnp.einsum('stcr,psc->tpr', values, phase_table, precision=highest, prefe...  8.17 us
  transfers between devices with their start and end apart: 4, of which 4 were waited for; matrix products, arithmetic and copies ran while one was open for 7% of the time, Pallas kernels for 0%

commit v1 on v0

v1 whole, which is shorter than its diff:
```python
import functools
import math

import jax
import jax.numpy as jnp
from jax import lax
from jax.experimental import pallas as pl
from jax.experimental.pallas import tpu as pltpu
from jax.sharding import PartitionSpec as P

time_step = 0.5
filter_strength = 36.0
MESH = pl.DeviceIdType.MESH
F32 = jnp.float32
BF16 = jnp.bfloat16

LAT = 6
HALF = 768
NR = 128
PEERS = 128
DEG = 512
NTH = 768
GROUPS = 3 * PEERS
ROWS = 8 * GROUPS


def ring(count, k):
    return count // 2 + lax.div(k + 1, 2) * (1 - 2 * lax.rem(k, 2))


def peer_of(i, row, col):
    z, y, x = lax.rem(row, 8), 2 * lax.div(row, 8) + lax.div(col, 4), lax.rem(col, 4)
    z2 = lax.rem(z + ring(8, lax.rem(i, 8)), 8)
    x2 = lax.rem(x + ring(4, lax.rem(lax.div(i, 8), 4)), 4)
    y2 = lax.rem(y + ring(4, lax.div(i, 32)), 4)
    return 8 * lax.div(y2, 2) + z2, 4 * lax.rem(y2, 2) + x2


def wave(order, longitude):
    longitudes = 2 * HALF
    phase = order * longitude
    turns = jnp.round(phase * (1.0 / longitudes))
    angle = (phase - turns * longitudes) * (math.pi / longitudes)
    square = angle * angle
    sine = angle * (1.0 + square * (-1 / 6 + square * (1 / 120 + square * (-1 / 5040 + square * (1 / 362880)))))
    cosine = 1.0 + square * (
        -1 / 2 + square * (1 / 24 + square * (-1 / 720 + square * (1 / 40320 - square * (1 / 3628800))))
    )
    scale = 1.0 / math.sqrt(longitudes)
    return scale - (2.0 * scale) * sine * sine, (-2.0 * scale) * sine * cosine


def dot(a, b):
    return jnp.dot(a, b, preferred_element_type=F32)


def kernel(
    order_ref, orders_ref, kappa_ref, right_ref, left_ref, grid_hbm, legendre_hbm, state_hbm,
    evolved_ref, new_ref,
    grid, grid_out, grid_in, table, table_t, wide, pack_a, got_a, pack_b, got_b, legendre, legendre_t,
    state, columns, factor, part_out, part_in,
    load_sem, send_sem, recv_sem,
):
    sec, row, col = lax.axis_index("sec"), lax.axis_index("row"), lax.axis_index("col")
    me = 8 * row + col
    partner = (1 - sec, row, col)
    sign = (1 - 2 * sec).astype(F32)

    loads = [pltpu.make_async_copy(grid_hbm.at[t], grid.at[t], load_sem.at[t]) for t in range(LAT)]
    loads.append(pltpu.make_async_copy(legendre_hbm.at[0], legendre, load_sem.at[LAT]))
    loads.append(pltpu.make_async_copy(state_hbm.at[0], state, load_sem.at[LAT + 1]))
    for load in loads:
        load.start()

    barrier = pltpu.get_barrier_semaphore()

    def greet(i, _):
        row2, col2 = peer_of(i, row, col)
        pl.semaphore_signal(barrier, inc=1, device_id=(sec, row2, col2), device_id_type=MESH)
        return 0

    pl.semaphore_signal(barrier, inc=1, device_id=partner, device_id_type=MESH)
    lax.fori_loop(0, PEERS - 1, greet, 0)

    for t in range(LAT):
        loads[t].wait()
        grid_out[t] = grid[t].astype(BF16)

    low = orders_ref[pl.ds(sec, 1), :]
    even = jnp.where(lax.rem(low, 2) == 0, low, DEG - 1 - low).astype(F32)
    even_t = jnp.transpose(jnp.broadcast_to(even, (PEERS, PEERS)))

    pl.semaphore_wait(barrier, PEERS)

    def give(t):
        return pltpu.make_async_remote_copy(
            grid_out.at[t], grid_in.at[t], send_sem.at[t], recv_sem.at[t], device_id=partner, device_id_type=MESH
        )

    for t in range(LAT):
        give(t).start()

    for lane in range(HALF // 128):
        longitude = (lax.broadcasted_iota(jnp.int32, (PEERS, 128), 1) + 128 * lane).astype(F32)
        for parity in range(2):
            order = even_t if parity == 0 else (DEG - 1.0) - even_t
            real, imag = wave(order, longitude)
            if parity == 1:
                real, imag = real * sign, imag * sign
            span = pl.ds(128 * lane, 128)
            table[parity, 0:PEERS, span] = real.astype(BF16)
            table[parity, PEERS : 2 * PEERS, span] = imag.astype(BF16)

    for k in range(LAT // 2):
        give(2 * k).wait_recv()
        give(2 * k + 1).wait_recv()
        for parity in range(2):
            values = []
            for t in (2 * k, 2 * k + 1):
                other = grid_in[t].astype(F32)
                values.append((grid[t] + other if parity == 0 else grid[t] - other).astype(BF16))
            sums = dot(table[parity], jnp.concatenate(values, axis=1))
            for c in range(2):
                for j in range(2):
                    at = (2 * k + j) * 4 + 2 * parity + c
                    wide[pl.ds(at, PEERS, stride=24), :] = sums[c * PEERS : (c + 1) * PEERS, j * NR : (j + 1) * NR]
    for t in range(LAT):
        give(t).wait_send()

    def narrow(pack):
        def body(i, _):
            pack[pl.ds(32 * i, 32)] = wide[pl.ds(256 * i, 256), :].reshape(32, 8, NR).astype(BF16)
            return 0

        lax.fori_loop(0, GROUPS // 32, body, 0)

    def widen(got):
        def body(i, _):
            wide[pl.ds(256 * i, 256), :] = got[pl.ds(32 * i, 32)].astype(F32).reshape(256, NR)
            return 0

        lax.fori_loop(0, GROUPS // 32, body, 0)

    def exchange(pack, got, sem):
        def body(i, _):
            row2, col2 = peer_of(i, row, col)
            pltpu.make_async_remote_copy(
                pack.at[pl.ds(3 * (8 * row2 + col2), 3)], got.at[pl.ds(3 * me, 3)],
                send_sem.at[sem], recv_sem.at[sem], device_id=(sec, row2, col2), device_id_type=MESH,
            ).start()
            return 0

        lax.fori_loop(0, PEERS - 1, body, 0)
        got[pl.ds(3 * me, 3)] = pack[pl.ds(3 * me, 3)]

    def finish(pack, got, sem):
        count = 3 * (PEERS - 1)
        both = pltpu.make_async_remote_copy(
            pack.at[pl.ds(0, count)], got.at[pl.ds(0, count)], send_sem.at[sem], recv_sem.at[sem],
            device_id=partner, device_id_type=MESH,
        )
        both.wait_recv()
        both.wait_send()

    narrow(pack_a)
    exchange(pack_a, got_a, LAT)

    for lane in range(HALF // 128):
        longitude = (lax.broadcasted_iota(jnp.int32, (128, PEERS), 0) + 128 * lane).astype(F32)
        for parity in range(2):
            order = jnp.broadcast_to(even if parity == 0 else (DEG - 1.0) - even, (128, PEERS))
            real, imag = wave(order, longitude)
            if parity == 1:
                real, imag = real * sign, imag * sign
            span = pl.ds(128 * lane, 128)
            table_t[parity, span, 0:PEERS] = real.astype(BF16)
            table_t[parity, span, PEERS : 2 * PEERS] = imag.astype(BF16)
    loads[LAT].wait()
    loads[LAT + 1].wait()
    for i in range(4):
        for j in range(6):
            legendre_t[pl.ds(128 * j, 128), pl.ds(128 * i, 128)] = jnp.transpose(
                legendre[pl.ds(128 * i, 128), pl.ds(128 * j, 128)].astype(F32)
            ).astype(BF16)
    mine = order_ref[PEERS * sec + me]
    index = lax.broadcasted_iota(jnp.int32, (DEG + 1, NR), 0)
    leading = index < DEG - mine
    degree = jnp.where(leading, mine + index, index - 1).astype(F32)
    mode = lax.broadcasted_iota(jnp.int32, (1, NR), 1).astype(F32) * (1.0 / NR)
    mode4 = (mode * mode) * (mode * mode)
    mode8 = mode4 * mode4
    mode16 = mode8 * mode8
    damping = jnp.exp(-filter_strength * (mode16 * mode16 * mode4))
    factor[...] = damping / (1.0 + kappa_ref[...] + degree * (degree + 1.0) * (1.0 / (DEG * DEG)))

    finish(pack_a, got_a, LAT)

    widen(got_a)
    for q in range(4):
        columns[:, q * NR : (q + 1) * NR] = wide[pl.ds(q, NTH, stride=4), :].astype(BF16)
    both = dot(legendre[...], columns[...])
    index = lax.broadcasted_iota(jnp.int32, (DEG + 1, 2 * NR), 0)
    first = (index < DEG - mine) == (lax.rem(mine, 2) == 0)
    coefficient = jnp.where(first, both[:, : 2 * NR], both[:, 2 * NR :])
    right_side = (state[...].astype(F32) + time_step * coefficient).astype(BF16)
    parts = []
    for c in range(2):
        eigen = dot(right_side[:, c * NR : (c + 1) * NR], right_ref[...])
        scaled = (eigen * factor[...]).astype(BF16)
        parts.append(dot(scaled, left_ref[...]))
    new_wide = jnp.concatenate(parts, axis=1)
    new_ref[0] = new_wide.astype(BF16)
    new_wide = new_wide.astype(BF16).astype(F32)
    split = jnp.concatenate([jnp.where(first, new_wide, 0.0), jnp.where(first, 0.0, new_wide)], axis=1)
    tail = split[DEG:, :]
    main = split[:DEG, :].astype(BF16)
    ends = legendre[DEG:, :].astype(F32)
    tail_t = jnp.transpose(jnp.broadcast_to(ends, (128, NTH)))
    for q in range(4):
        span = slice(q * NR, (q + 1) * NR)
        wide[pl.ds(q, NTH, stride=4), :] = dot(legendre_t[...], main[:, span]) + tail_t * tail[:, span]
    narrow(pack_b)
    exchange(pack_b, got_b, LAT + 1)
    finish(pack_b, got_b, LAT + 1)
    widen(got_b)

    def pass_on(t):
        return pltpu.make_async_remote_copy(
            part_out.at[t], part_in.at[t], send_sem.at[LAT + 2 + t], recv_sem.at[LAT + 2 + t],
            device_id=partner, device_id_type=MESH,
        )

    for k in range(LAT // 2):
        sums = []
        for parity in range(2):
            halves = []
            for j in range(2):
                at = (2 * k + j) * 4 + 2 * parity
                halves.append(
                    jnp.concatenate(
                        [wide[pl.ds(at + c, PEERS, stride=24), :].astype(BF16) for c in range(2)], axis=0
                    )
                )
            sums.append(dot(table_t[parity], jnp.concatenate(halves, axis=1)))
        keep, other = sums[0] + sums[1], (sums[0] - sums[1]).astype(BF16)
        for j in range(2):
            t = 2 * k + j
            evolved_ref[t] = keep[:, j * NR : (j + 1) * NR]
            part_out[t] = other[:, j * NR : (j + 1) * NR]
            pass_on(t).start()
    for t in range(LAT):
        pass_on(t).wait_recv()
        evolved_ref[t] = evolved_ref[t] + part_in[t].astype(F32)
    for t in range(LAT):
        pass_on(t).wait_send()


def on_device(grid_terms, pair_orders, legendre, state, kappa, right_op, left_op):
    vmem = pl.BlockSpec(memory_space=pltpu.VMEM)
    anywhere = pl.BlockSpec(memory_space=pl.ANY)
    smem = pl.BlockSpec(memory_space=pltpu.SMEM)
    sems = 2 * LAT + 2
    evolved, new_state = pl.pallas_call(
        kernel,
        out_shape=(
            jax.ShapeDtypeStruct((LAT, HALF, NR), F32),
            jax.ShapeDtypeStruct((1, DEG + 1, 2 * NR), BF16),
        ),
        in_specs=[smem, vmem, vmem, vmem, vmem, anywhere, anywhere, anywhere],
        out_specs=(vmem, vmem),
        scratch_shapes=[
            pltpu.VMEM((LAT, HALF, NR), F32),
            pltpu.VMEM((LAT, HALF, NR), BF16),
            pltpu.VMEM((LAT, HALF, NR), BF16),
            pltpu.VMEM((2, 2 * PEERS, HALF), BF16),
            pltpu.VMEM((2, HALF, 2 * PEERS), BF16),
            pltpu.VMEM((ROWS, NR), F32),
            pltpu.VMEM((GROUPS, 8, NR), BF16),
            pltpu.VMEM((GROUPS, 8, NR), BF16),
            pltpu.VMEM((GROUPS, 8, NR), BF16),
            pltpu.VMEM((GROUPS, 8, NR), BF16),
            pltpu.VMEM((DEG + 1, NTH), BF16),
            pltpu.VMEM((NTH, DEG), BF16),
            pltpu.VMEM((DEG + 1, 2 * NR), BF16),
            pltpu.VMEM((NTH, 4 * NR), BF16),
            pltpu.VMEM((DEG + 1, NR), F32),
            pltpu.VMEM((LAT, HALF, NR), BF16),
            pltpu.VMEM((LAT, HALF, NR), BF16),
            pltpu.SemaphoreType.DMA((LAT + 2,)),
            pltpu.SemaphoreType.DMA((sems,)),
            pltpu.SemaphoreType.DMA((sems,)),
        ],
        compiler_params=pltpu.CompilerParams(
            collective_id=0, has_side_effects=True, vmem_limit_bytes=60 * 1024 * 1024
        ),
    )(
        pair_orders,
        pair_orders.reshape(2, PEERS),
        kappa.reshape(1, NR),
        right_op,
        left_op,
        grid_terms,
        legendre,
        state,
    )
    return evolved, new_state


def solution(mesh):
    return jax.shard_map(
        on_device,
        mesh=mesh,
        in_specs=(
            P(("row", "col"), "sec", None),
            P(),
            P(("sec", "row", "col"), None, None),
            P(("sec", "row", "col"), None, None),
            P(),
            P(),
            P(),
        ),
        out_specs=(P(("row", "col"), "sec", None), P(("sec", "row", "col"), None, None)),
        check_vma=False,
    )
```

time: 166 us -> 71.8 us (0.43)
  waiting for transfers between devices: 74.2 us -> 0 us
  Pallas kernels: 0 us -> 66.9 us
  other arithmetic: 21.6 us -> 0 us
  starting transfers between devices: 20.5 us -> 0 us
  matrix products: 19.7 us -> 0 us
  between operations: 14.9 us -> 0.65 us
  local copies, waits for them, and re-layouts: 14.5 us -> 3.97 us
    pallas_call x0 -> x1, Pallas kernels: none -> 66.9 us  [on_device(): pl.pallas_call(kernel, out_shape=(jax.ShapeDtypeStruct((LAT, HALF, NR), F...]
    all_to_all x2 -> x0, waiting for transfers between devices: 42 us -> none  [the longest x1 27.5 us: on_device(): lax.all_to_all(spectral, ('row', 'col'), split_axis=0, concat_axis=1, til...]
    reduce_scatter x2 -> x0, waiting for transfers between devices: 32.2 us -> none  [the longest x1 20.4 us: on_device(): lax.psum_scatter(term.reshape(section_slots * lax.axis_size('sec'), lat_r...]
    all_to_all x2 -> x0, starting transfers between devices: 20.2 us -> none  [the longest x1 14.1 us: on_device(): lax.all_to_all(spectral, ('row', 'col'), split_axis=0, concat_axis=1, til...]
    dot_general x5 -> x0, matrix products: 19.7 us -> none  [the longest x1 8.4 us: on_device(): jnp.einsum('tpr,psc->stcr', grid_terms, phase_table, precision=highest, p...]
    mul x2 -> x0, other arithmetic: 14 us -> none  [fourier_table(): jnp.cos(phase_angle) * norm_scale]
    reshape x5 -> x0, local copies, waits for them, and re-layouts: 6.43 us -> none  [the longest x1 2.9 us: on_device(): returned.astype(jnp.float32).reshape(section_slots, lat_rows, 2, radial)]
    convert_element_type x3 -> x0, other arithmetic: 4.48 us -> none  [the longest x1 2.83 us: on_device(): evolved = lax.psum_scatter(partial_value.astype(jnp.bfloat16), 'sec', sca...]
  transfers between devices with their start and end apart: 4 -> 0, of which waited for: 4 -> 0; matrix products, arithmetic and copies ran while one was open for 7% -> 0% of each run, Pallas kernels for 0% -> 0%
where the time goes in v1:
time: 71.8 us; the launch traced here: 71.6 us
  Pallas kernels  66.9 us (93%)
  local copies, waits for them, and re-layouts  3.97 us (6%)
    pallas_call x1, Pallas kernels, on_device(): pl.pallas_call(kernel, out_shape=(jax.ShapeDtypeStruct((LAT, HALF, NR), F...  66.9 us
    unnamed x4, local copies, waits for them, and re-layouts  3.97 us

profile of v1, /device:TPU:1, one launch (start us, length us, event | category | flops | bytes accessed | tf_op | source)
XLA Modules:
  0.0 71.6 jit_solution(18257012979989555023)
XLA Ops:
  0.6 66.9 %shard_map.86 = (f32[6,768,128]{2,1,0:T(8,128)}, bf16[1,513,256]{2,1,0:T(8,128)(2,1)}) custom-call(s32[256]{0:T(256)} %order_ref.1, s32[2,128]{1,0:T(2,128)} %bitcast.2, f32[1,128]{1,0:T(1,128)} %bitcast.3, bf16[128,128]{1,0:T(8,128)(2,1)} %right_ref.1, bf16[128,128]{1,0:T(8,128)(2,1)} %left_ref.1, f32[6,768,128]{2,1,0:T(8,128)} %grid_hbm.1, ...), custom_call_target="tpu_custom_call" | custom-call | tf_op jit(solution)/shard_map/pallas_call | solution.py:263
  67.6 0.0 copy-start
  67.6 3.3 %copy.11 = f32[6,768,128]{2,1,0:T(8,128)} copy(f32[6,768,128]{2,1,0:T(8,128)} %get-tuple-element.4) | data formatting | bytes 4718592
  70.9 0.0 copy-done
  70.9 0.7 copy.12
Async XLA Ops:
  67.6 3.3 %copy-start = (bf16[1,513,256]{2,1,0:T(8,128)(2,1)S(1)}, bf16[1,513,256]{2,1,0:T(8,128)(2,1)}, u32[]{:S(2)}) copy-start(bf16[1,513,256]{2,1,0:T(8,128)(2,1)} %get-tuple-element.5) | copy-start | bytes 787972

commit v2 on v1

v2 whole, which is shorter than its diff:
```python
import functools
import math

import jax
import jax.numpy as jnp
from jax import lax
from jax.experimental import pallas as pl
from jax.experimental.pallas import tpu as pltpu
from jax.sharding import PartitionSpec as P

time_step = 0.5
filter_strength = 36.0
MESH = pl.DeviceIdType.MESH
F32 = jnp.float32
BF16 = jnp.bfloat16

LAT = 6
HALF = 768
NR = 128
PEERS = 128
DEG = 512
NTH = 768


def ring(count, k):
    return count // 2 + lax.div(k + 1, 2) * (1 - 2 * lax.rem(k, 2))


def peer_of(i, row, col):
    z, y, x = lax.rem(row, 8), 2 * lax.div(row, 8) + lax.div(col, 4), lax.rem(col, 4)
    z2 = lax.rem(z + ring(8, lax.rem(i, 8)), 8)
    x2 = lax.rem(x + ring(4, lax.rem(lax.div(i, 8), 4)), 4)
    y2 = lax.rem(y + ring(4, lax.div(i, 32)), 4)
    return 8 * lax.div(y2, 2) + z2, 4 * lax.rem(y2, 2) + x2


def wave(order, longitude):
    longitudes = 2 * HALF
    phase = order * longitude
    turns = jnp.round(phase * (1.0 / longitudes))
    angle = (phase - turns * longitudes) * (math.pi / longitudes)
    square = angle * angle
    sine = angle * (1.0 + square * (-1 / 6 + square * (1 / 120 + square * (-1 / 5040 + square * (1 / 362880)))))
    cosine = 1.0 + square * (
        -1 / 2 + square * (1 / 24 + square * (-1 / 720 + square * (1 / 40320 - square * (1 / 3628800))))
    )
    scale = 1.0 / math.sqrt(longitudes)
    return scale - (2.0 * scale) * sine * sine, (-2.0 * scale) * sine * cosine


def dot(a, b):
    return jnp.dot(a, b, preferred_element_type=F32)


def kernel(
    orders_hbm, kappa_hbm, right_hbm, left_hbm, grid_hbm, legendre_hbm, state_hbm,
    keep_ref, part_in, new_ref,
    orders_s, orders_v, kappa, right, left,
    grid, grid_out, grid_in, table, table_t,
    wide_a0, wide_a1, wide_b0, wide_b1, pack_a0, pack_a1, pack_b0, pack_b1, got_a0, got_a1, got_b0, got_b1,
    legendre, permute, rows, rows_t, state, columns, factor, part_out,
    load_sem, send_sem, recv_sem,
):
    sec, row, col = lax.axis_index("sec"), lax.axis_index("row"), lax.axis_index("col")
    me = 8 * row + col
    partner = (1 - sec, row, col)
    sign = (1 - 2 * sec).astype(F32)

    loads = [pltpu.make_async_copy(grid_hbm.at[t], grid.at[t], load_sem.at[t]) for t in range(LAT)]
    for source, target in (
        (orders_hbm, orders_v), (orders_hbm, orders_s), (legendre_hbm.at[0], legendre), (state_hbm.at[0], state),
        (kappa_hbm, kappa), (right_hbm, right), (left_hbm, left),
    ):
        loads.append(pltpu.make_async_copy(source, target, load_sem.at[len(loads)]))
    for load in loads:
        load.start()

    barrier = pltpu.get_barrier_semaphore()

    def greet(i, _):
        row2, col2 = peer_of(i, row, col)
        pl.semaphore_signal(barrier, inc=1, device_id=(sec, row2, col2), device_id_type=MESH)
        return 0

    pl.semaphore_signal(barrier, inc=1, device_id=partner, device_id_type=MESH)
    lax.fori_loop(0, PEERS - 1, greet, 0)

    for t in range(LAT):
        loads[t].wait()
        grid_out[t] = grid[t].astype(BF16)

    loads[LAT].wait()
    low = orders_v[pl.ds(sec, 1), :]
    even = jnp.where(lax.rem(low, 2) == 0, low, DEG - 1 - low).astype(F32)
    even_t = jnp.transpose(jnp.broadcast_to(even, (PEERS, PEERS)))

    pl.semaphore_wait(barrier, PEERS)

    def give(t):
        return pltpu.make_async_remote_copy(
            grid_out.at[t], grid_in.at[t], send_sem.at[t], recv_sem.at[t], device_id=partner, device_id_type=MESH
        )

    for t in range(LAT):
        give(t).start()

    for lane in range(HALF // 128):
        longitude = (lax.broadcasted_iota(jnp.int32, (PEERS, 128), 1) + 128 * lane).astype(F32)
        for parity in range(2):
            order = even_t if parity == 0 else (DEG - 1.0) - even_t
            real, imag = wave(order, longitude)
            if parity == 1:
                real, imag = real * sign, imag * sign
            span = pl.ds(128 * lane, 128)
            table[parity, 0:PEERS, span] = real.astype(BF16)
            table[parity, PEERS : 2 * PEERS, span] = imag.astype(BF16)

    def there(c, parity, t):
        at = 12 * c + 6 * parity + t
        return (wide_a0, pl.ds(at, PEERS, stride=16)) if at < 16 else (wide_a1, pl.ds(at - 16, PEERS, stride=8))

    def back(c, parity, t):
        at = 12 * c + 6 * parity + t
        return (wide_b0, pl.ds(at, PEERS, stride=8)) if at < 8 else (wide_b1, pl.ds(at - 8, PEERS, stride=16))

    for k in range(LAT // 2):
        give(2 * k).wait_recv()
        give(2 * k + 1).wait_recv()
        for parity in range(2):
            values = []
            for t in (2 * k, 2 * k + 1):
                other = grid_in[t].astype(F32)
                values.append((grid[t] + other if parity == 0 else grid[t] - other).astype(BF16))
            sums = dot(table[parity], jnp.concatenate(values, axis=1))
            for c in range(2):
                for j in range(2):
                    wide, span = there(c, parity, 2 * k + j)
                    wide[span, :] = sums[c * PEERS : (c + 1) * PEERS, j * NR : (j + 1) * NR]
    for t in range(LAT):
        give(t).wait_send()

    def narrow(wide, pack):
        def body(i, _):
            pack[pl.ds(32 * i, 32)] = wide[pl.ds(256 * i, 256), :].reshape(32, 8, NR).astype(BF16)
            return 0

        lax.fori_loop(0, pack.shape[0] // 32, body, 0)

    def widen(got, wide):
        def body(i, _):
            wide[pl.ds(256 * i, 256), :] = got[pl.ds(32 * i, 32)].astype(F32).reshape(256, NR)
            return 0

        lax.fori_loop(0, got.shape[0] // 32, body, 0)

    def exchange(pack, got, sem):
        tiles = pack.shape[0] // PEERS

        def body(i, _):
            row2, col2 = peer_of(i, row, col)
            pltpu.make_async_remote_copy(
                pack.at[pl.ds(tiles * (8 * row2 + col2), tiles)], got.at[pl.ds(tiles * me, tiles)],
                send_sem.at[sem], recv_sem.at[sem], device_id=(sec, row2, col2), device_id_type=MESH,
            ).start()
            return 0

        lax.fori_loop(0, PEERS - 1, body, 0)
        got[pl.ds(tiles * me, tiles)] = pack[pl.ds(tiles * me, tiles)]

    def whole(pack, got, sem):
        count = pack.shape[0] // PEERS * (PEERS - 1)
        return pltpu.make_async_remote_copy(
            pack.at[pl.ds(0, count)], got.at[pl.ds(0, count)], send_sem.at[sem], recv_sem.at[sem],
            device_id=partner, device_id_type=MESH,
        )

    narrow(wide_a0, pack_a0)
    exchange(pack_a0, got_a0, LAT)
    narrow(wide_a1, pack_a1)
    exchange(pack_a1, got_a1, LAT + 1)

    for load in loads[LAT + 1 :]:
        load.wait()
    for lane in range(HALF // 128):
        longitude = (lax.broadcasted_iota(jnp.int32, (128, PEERS), 0) + 128 * lane).astype(F32)
        for parity in range(2):
            order = jnp.broadcast_to(even if parity == 0 else (DEG - 1.0) - even, (128, PEERS))
            real, imag = wave(order, longitude)
            if parity == 1:
                real, imag = real * sign, imag * sign
            span = pl.ds(128 * lane, 128)
            table_t[parity, span, 0:PEERS] = real.astype(BF16)
            table_t[parity, span, PEERS : 2 * PEERS] = imag.astype(BF16)
    for t in range(LAT):
        latitude = lax.broadcasted_iota(jnp.int32, (NTH, PEERS), 0)
        device = lax.broadcasted_iota(jnp.int32, (NTH, PEERS), 1)
        permute[:, t * PEERS : (t + 1) * PEERS] = jnp.where(latitude == LAT * device + t, 1.0, 0.0).astype(BF16)
    rows[...] = dot(legendre[...], permute[...]).astype(BF16)
    for i in range(4):
        for j in range(LAT):
            rows_t[pl.ds(128 * j, 128), pl.ds(128 * i, 128)] = jnp.transpose(
                rows[pl.ds(128 * i, 128), pl.ds(128 * j, 128)].astype(F32)
            ).astype(BF16)
    mine = orders_s[sec, me]
    index = lax.broadcasted_iota(jnp.int32, (DEG + 1, NR), 0)
    leading = index < DEG - mine
    first = leading == (lax.rem(mine, 2) == 0)
    degree = jnp.where(leading, mine + index, index - 1).astype(F32)
    mode = lax.broadcasted_iota(jnp.int32, (1, NR), 1).astype(F32) * (1.0 / NR)
    mode4 = (mode * mode) * (mode * mode)
    mode8 = mode4 * mode4
    mode16 = mode8 * mode8
    damping = jnp.exp(-filter_strength * (mode16 * mode16 * mode4))
    factor[...] = damping / (1.0 + kappa[...] + degree * (degree + 1.0) * (1.0 / (DEG * DEG)))

    for c in range(2):
        if c == 0:
            whole(pack_a0, got_a0, LAT).wait_recv()
            widen(got_a0, wide_a0)
        else:
            whole(pack_a1, got_a1, LAT + 1).wait_recv()
            widen(got_a1, wide_a1)
        for parity in range(2):
            for t in range(LAT):
                wide, span = there(c, parity, t)
                columns[t * PEERS : (t + 1) * PEERS, parity * NR : (parity + 1) * NR] = wide[span, :].astype(BF16)
        both = dot(rows[...], columns[...])
        coefficient = jnp.where(first, both[:, :NR], both[:, NR:])
        right_side = state[:, c * NR : (c + 1) * NR].astype(F32) + time_step * coefficient
        scaled = (dot(right_side.astype(BF16), right[...]) * factor[...]).astype(BF16)
        new = dot(scaled, left[...]).astype(BF16)
        new_ref[0, :, c * NR : (c + 1) * NR] = new
        new = new.astype(F32)
        split = jnp.concatenate([jnp.where(first, new, 0.0), jnp.where(first, 0.0, new)], axis=1)
        tail = split[DEG:, :]
        ends = jnp.transpose(jnp.broadcast_to(rows[DEG:, :].astype(F32), (128, NTH)))
        ends = jnp.concatenate([ends, ends], axis=1)
        sums = dot(rows_t[...], split[:DEG, :].astype(BF16)) + ends * tail
        for parity in range(2):
            for t in range(LAT):
                wide, span = back(c, parity, t)
                wide[span, :] = sums[t * PEERS : (t + 1) * PEERS, parity * NR : (parity + 1) * NR]
        if c == 0:
            narrow(wide_b0, pack_b0)
            exchange(pack_b0, got_b0, LAT + 2)
        else:
            narrow(wide_b1, pack_b1)
            exchange(pack_b1, got_b1, LAT + 3)

    whole(pack_a0, got_a0, LAT).wait_send()
    whole(pack_a1, got_a1, LAT + 1).wait_send()
    whole(pack_b0, got_b0, LAT + 2).wait_recv()
    widen(got_b0, wide_b0)
    whole(pack_b1, got_b1, LAT + 3).wait_recv()
    widen(got_b1, wide_b1)

    def pass_on(t):
        return pltpu.make_async_remote_copy(
            part_out.at[t], part_in.at[t], send_sem.at[LAT + 4 + t], recv_sem.at[LAT + 4 + t],
            device_id=partner, device_id_type=MESH,
        )

    for k in range(LAT // 2):
        sums = []
        for parity in range(2):
            halves = []
            for t in (2 * k, 2 * k + 1):
                pieces = []
                for c in range(2):
                    wide, span = back(c, parity, t)
                    pieces.append(wide[span, :].astype(BF16))
                halves.append(jnp.concatenate(pieces, axis=0))
            sums.append(dot(table_t[parity], jnp.concatenate(halves, axis=1)))
        keep, other = sums[0] + sums[1], (sums[0] - sums[1]).astype(BF16)
        for j in range(2):
            t = 2 * k + j
            part_out[t] = other[:, j * NR : (j + 1) * NR]
            pass_on(t).start()
            keep_ref[t] = keep[:, j * NR : (j + 1) * NR]
    for t in range(LAT):
        pass_on(t).wait_recv()
    whole(pack_b0, got_b0, LAT + 2).wait_send()
    whole(pack_b1, got_b1, LAT + 3).wait_send()
    for t in range(LAT):
        pass_on(t).wait_send()


def join(keep_ref, part_ref, new_ref, evolved_hbm, new_hbm, total, sem):
    copies = [pltpu.make_async_copy(new_ref, new_hbm, sem.at[LAT])]
    copies[0].start()
    for t in range(LAT):
        total[t] = keep_ref[t] + part_ref[t].astype(F32)
        copies.append(pltpu.make_async_copy(total.at[t], evolved_hbm.at[t], sem.at[t]))
        copies[-1].start()
    for copy in copies:
        copy.wait()


def on_device(grid_terms, pair_orders, legendre, state, kappa, right_op, left_op):
    vmem = pl.BlockSpec(memory_space=pltpu.VMEM)
    hbm = pl.BlockSpec(memory_space=pltpu.HBM)
    sems = 2 * LAT + 4
    mib = 1024 * 1024
    grid_shape = (LAT, HALF, NR)
    keep, part, new_state = pl.pallas_call(
        kernel,
        out_shape=(
            jax.ShapeDtypeStruct(grid_shape, F32),
            jax.ShapeDtypeStruct(grid_shape, BF16),
            jax.ShapeDtypeStruct((1, DEG + 1, 2 * NR), BF16),
        ),
        in_specs=[hbm] * 7,
        out_specs=(vmem, vmem, vmem),
        scratch_shapes=[
            pltpu.SMEM((2, PEERS), jnp.int32),
            pltpu.VMEM((2, PEERS), jnp.int32),
            pltpu.VMEM((1, NR), F32),
            pltpu.VMEM((NR, NR), BF16),
            pltpu.VMEM((NR, NR), BF16),
            pltpu.VMEM(grid_shape, F32),
            pltpu.VMEM(grid_shape, BF16),
            pltpu.VMEM(grid_shape, BF16),
            pltpu.VMEM((2, 2 * PEERS, HALF), BF16),
            pltpu.VMEM((2, HALF, 2 * PEERS), BF16),
        ]
        + [pltpu.VMEM((rows * PEERS, NR), F32) for rows in (16, 8, 8, 16)]
        + [pltpu.VMEM((tiles * PEERS, 8, NR), BF16) for tiles in (2, 1, 1, 2)] * 2
        + [
            pltpu.VMEM((DEG + 1, NTH), BF16),
            pltpu.VMEM((NTH, NTH), BF16),
            pltpu.VMEM((DEG + 1, NTH), BF16),
            pltpu.VMEM((NTH, DEG), BF16),
            pltpu.VMEM((DEG + 1, 2 * NR), BF16),
            pltpu.VMEM((NTH, 2 * NR), BF16),
            pltpu.VMEM((DEG + 1, NR), F32),
            pltpu.VMEM(grid_shape, BF16),
            pltpu.SemaphoreType.DMA((LAT + 7,)),
            pltpu.SemaphoreType.DMA((sems,)),
            pltpu.SemaphoreType.DMA((sems,)),
        ],
        compiler_params=pltpu.CompilerParams(collective_id=0, has_side_effects=True, vmem_limit_bytes=36 * mib),
    )(
        *(
            pltpu.with_memory_space_constraint(array, pltpu.HBM)
            for array in (
                pair_orders.reshape(2, PEERS), kappa.reshape(1, NR), right_op, left_op, grid_terms, legendre, state,
            )
        )
    )
    return pl.pallas_call(
        join,
        out_shape=(
            jax.ShapeDtypeStruct(grid_shape, F32),
            jax.ShapeDtypeStruct((1, DEG + 1, 2 * NR), BF16),
        ),
        in_specs=[vmem, vmem, vmem],
        out_specs=(hbm, hbm),
        scratch_shapes=[pltpu.VMEM(grid_shape, F32), pltpu.SemaphoreType.DMA((LAT + 1,))],
        compiler_params=pltpu.CompilerParams(vmem_limit_bytes=16 * mib),
    )(keep, part, new_state)


def solution(mesh):
    return jax.shard_map(
        on_device,
        mesh=mesh,
        in_specs=(
            P(("row", "col"), "sec", None),
            P(),
            P(("sec", "row", "col"), None, None),
            P(("sec", "row", "col"), None, None),
            P(),
            P(),
            P(),
        ),
        out_specs=(P(("row", "col"), "sec", None), P(("sec", "row", "col"), None, None)),
        check_vma=False,
    )
```

time: 71.8 us -> 62.8 us (0.87)
  Pallas kernels: 66.9 us -> 62.1 us
  local copies, waits for them, and re-layouts: 3.97 us -> 0 us
    pallas_call x1 -> x2, Pallas kernels: 66.9 us -> 62.1 us  [the longest x1 60.5 us: on_device(): pl.pallas_call(kernel, out_shape=(jax.ShapeDtypeStruct(grid_shape, F32),...]
    unnamed x4 -> x0, local copies, waits for them, and re-layouts: 3.97 us -> none
where the time goes in v2:
time: 62.8 us; the launch traced here: 62.7 us
  Pallas kernels  62.1 us (99%)
  between operations  0.64 us (1%)
    pallas_call x1, Pallas kernels, on_device(): pl.pallas_call(kernel, out_shape=(jax.ShapeDtypeStruct(grid_shape, F32),...  60.5 us
    pallas_call x1, Pallas kernels, on_device(): pl.pallas_call(join, out_shape=(jax.ShapeDtypeStruct(grid_shape, F32), ja...  1.54 us

profile of v2, /device:TPU:1, one launch (start us, length us, event | category | flops | bytes accessed | tf_op | source)
XLA Modules:
  0.0 62.7 jit_solution(7817662160750007832)
XLA Ops:
  0.6 60.5 %shard_map.86 = (f32[6,768,128]{2,1,0:T(8,128)S(1)}, bf16[6,768,128]{2,1,0:T(8,128)(2,1)S(1)}, bf16[1,513,256]{2,1,0:T(8,128)(2,1)S(1)}) custom-call(s32[2,128]{1,0:T(2,128)} %bitcast.2, f32[1,128]{1,0:T(1,128)} %bitcast.3, bf16[128,128]{1,0:T(8,128)(2,1)} %right_hbm.1, bf16[128,128]{1,0:T(8,128)(2,1)} %left_hbm.1, f32[6,768,128]{2,1,0:T(8,128)} %grid_hbm.1, ...), custom_call_target="tpu_custom_call" | custom-call | tf_op jit(solution)/shard_map/pallas_call | solution.py:305
  61.2 1.5 %shard_map.87 = (f32[6,768,128]{2,1,0:T(8,128)}, bf16[1,513,256]{2,1,0:T(8,128)(2,1)}) custom-call(f32[6,768,128]{2,1,0:T(8,128)S(1)} %get-tuple-element.5.keep_ref, bf16[6,768,128]{2,1,0:T(8,128)(2,1)S(1)} %get-tuple-element.6.part_ref, bf16[1,513,256]{2,1,0:T(8,128)(2,1)S(1)} %get-tuple-element.7.new_ref), custom_call_target="tpu_custom_call" | custom-call | tf_op jit(solution)/shard_map/pallas_call | solution.py:350

commit v3 on v2

v3 whole, which is shorter than its diff:
```python
import functools
import math

import jax
import jax.numpy as jnp
from jax import lax
from jax.experimental import pallas as pl
from jax.experimental.pallas import tpu as pltpu
from jax.sharding import PartitionSpec as P

time_step = 0.5
filter_strength = 36.0
MESH = pl.DeviceIdType.MESH
F32 = jnp.float32
BF16 = jnp.bfloat16

LAT = 6
HALF = 768
NR = 128
PEERS = 128
DEG = 512
NTH = 768


def ring(count, k):
    return count // 2 + lax.div(k + 1, 2) * (1 - 2 * lax.rem(k, 2))


def peer_of(i, row, col):
    z, y, x = lax.rem(row, 8), 2 * lax.div(row, 8) + lax.div(col, 4), lax.rem(col, 4)
    z2 = lax.rem(z + ring(8, lax.rem(i, 8)), 8)
    x2 = lax.rem(x + ring(4, lax.rem(lax.div(i, 8), 4)), 4)
    y2 = lax.rem(y + ring(4, lax.div(i, 32)), 4)
    return 8 * lax.div(y2, 2) + z2, 4 * lax.rem(y2, 2) + x2


def wave(order, longitude):
    longitudes = 2 * HALF
    phase = order * longitude
    turns = jnp.round(phase * (1.0 / longitudes))
    angle = (phase - turns * longitudes) * (math.pi / longitudes)
    square = angle * angle
    sine = angle * (1.0 + square * (-1 / 6 + square * (1 / 120 + square * (-1 / 5040 + square * (1 / 362880)))))
    cosine = 1.0 + square * (
        -1 / 2 + square * (1 / 24 + square * (-1 / 720 + square * (1 / 40320 - square * (1 / 3628800))))
    )
    scale = 1.0 / math.sqrt(longitudes)
    return scale - (2.0 * scale) * sine * sine, (-2.0 * scale) * sine * cosine


def dot(a, b):
    return jnp.dot(a, b, preferred_element_type=F32)


def kernel(
    orders_hbm, kappa_hbm, right_hbm, left_hbm, grid_hbm, legendre_hbm, state_hbm,
    sum_ref, table_other, passed_b0, passed_b1, new_ref,
    orders_s, orders_v, kappa, right, left,
    grid, grid_low, table, table_t,
    wide_a0, wide_a1, wide_b0, wide_b1, pack_a0, pack_a1, pack_b0, pack_b1, got_a0, got_a1, got_b0, got_b1,
    give_a0, give_a1, taken_a0, taken_a1,
    legendre, permute, rows, rows_t, state, columns, factor,
    load_sem, send_sem, recv_sem,
):
    sec, row, col = lax.axis_index("sec"), lax.axis_index("row"), lax.axis_index("col")
    me = 8 * row + col
    partner = (1 - sec, row, col)
    sign = (1 - 2 * sec).astype(F32)

    loads = [pltpu.make_async_copy(orders_hbm, orders_v, load_sem.at[0])]
    loads += [pltpu.make_async_copy(grid_hbm.at[t], grid.at[t], load_sem.at[t + 1]) for t in range(LAT)]
    for source, target in (
        (orders_hbm, orders_s), (legendre_hbm.at[0], legendre), (state_hbm.at[0], state),
        (kappa_hbm, kappa), (right_hbm, right), (left_hbm, left),
    ):
        loads.append(pltpu.make_async_copy(source, target, load_sem.at[len(loads)]))
    for load in loads:
        load.start()

    barrier = pltpu.get_barrier_semaphore()

    def greet(i, _):
        row2, col2 = peer_of(i, row, col)
        pl.semaphore_signal(barrier, inc=1, device_id=(sec, row2, col2), device_id_type=MESH)
        return 0

    pl.semaphore_signal(barrier, inc=1, device_id=partner, device_id_type=MESH)
    lax.fori_loop(0, PEERS - 1, greet, 0)

    loads[0].wait()
    evens = []
    for which in range(2):
        low = orders_v[pl.ds(sec if which == 0 else 1 - sec, 1), :]
        evens.append(jnp.where(lax.rem(low, 2) == 0, low, DEG - 1 - low).astype(F32))

    for which in range(2):
        even_t = jnp.transpose(jnp.broadcast_to(evens[which], (PEERS, PEERS)))
        real, imag = wave(even_t, lax.broadcasted_iota(jnp.int32, (PEERS, 128), 1).astype(F32))
        turn_real, turn_imag = wave(even_t, 128.0)
        turn_real, turn_imag = turn_real * math.sqrt(2 * HALF), turn_imag * math.sqrt(2 * HALF)
        for lane in range(HALF // 128):
            longitude = (lax.broadcasted_iota(jnp.int32, (8, 128), 1) + 128 * lane).astype(F32)
            last_real, last_imag = wave(jnp.full((8, 128), DEG - 1.0, F32), longitude)
            last_real = (last_real * (sign * math.sqrt(2 * HALF)))[:1]
            last_imag = (last_imag * (sign * math.sqrt(2 * HALF)))[:1]
            span = pl.ds(128 * lane, 128)
            table[which, 0:PEERS, span] = real.astype(BF16)
            table[which, PEERS : 2 * PEERS, span] = imag.astype(BF16)
            table[which, 2 * PEERS : 3 * PEERS, span] = (last_real * real + last_imag * imag).astype(BF16)
            table[which, 3 * PEERS :, span] = (last_imag * real - last_real * imag).astype(BF16)
            real, imag = real * turn_real - imag * turn_imag, imag * turn_real + real * turn_imag

    def there(c, parity, t):
        at = 12 * c + 6 * parity + t
        return (wide_a0, pl.ds(at, PEERS, stride=16)) if at < 16 else (wide_a1, pl.ds(at - 16, PEERS, stride=8))

    def narrow(wide, pack, added=None):
        def body(i, _):
            values = wide[pl.ds(256 * i, 256), :].reshape(32, 8, NR)
            if added is not None:
                values = values + added[pl.ds(32 * i, 32)].astype(F32)
            pack[pl.ds(32 * i, 32)] = values.astype(BF16)
            return 0

        lax.fori_loop(0, pack.shape[0] // 32, body, 0)

    for t in range(LAT):
        loads[t + 1].wait()
        grid_low[t] = grid[t].astype(BF16)
    for which in (1, 0):
        for k in range(LAT // 2):
            values = jnp.concatenate([grid_low[2 * k], grid_low[2 * k + 1]], axis=1)
            sums = dot(table[which], values)
            for parity in range(2):
                for c in range(2):
                    for j in range(2):
                        wide, span = there(c, parity, 2 * k + j)
                        at = (2 * parity + c) * PEERS
                        wide[span, :] = sums[at : at + PEERS, j * NR : (j + 1) * NR]
        if which == 1:
            narrow(wide_a0, give_a0)
            narrow(wide_a1, give_a1)

    pl.semaphore_wait(barrier, PEERS)

    def to_partner(source, target, sem):
        return pltpu.make_async_remote_copy(
            source, target, send_sem.at[sem], recv_sem.at[sem], device_id=partner, device_id_type=MESH
        )

    to_partner(give_a0, taken_a0, 0).start()
    to_partner(give_a1, taken_a1, 1).start()

    def exchange(pack, got, sem, start=0, stop=PEERS - 1):
        tiles = pack.shape[0] // PEERS

        def body(i, _):
            row2, col2 = peer_of(i, row, col)
            pltpu.make_async_remote_copy(
                pack.at[pl.ds(tiles * (8 * row2 + col2), tiles)], got.at[pl.ds(tiles * me, tiles)],
                send_sem.at[sem], recv_sem.at[sem], device_id=(sec, row2, col2), device_id_type=MESH,
            ).start()
            return 0

        lax.fori_loop(start, stop, body, 0)
        if stop == PEERS - 1:
            got[pl.ds(tiles * me, tiles)] = pack[pl.ds(tiles * me, tiles)]

    def whole(pack, got, sem, messages=PEERS - 1):
        count = pack.shape[0] // PEERS * messages
        return to_partner(pack.at[pl.ds(0, count)], got.at[pl.ds(0, count)], sem)

    to_partner(give_a0, taken_a0, 0).wait_recv()
    narrow(wide_a0, pack_a0, taken_a0)
    exchange(pack_a0, got_a0, 2)
    to_partner(give_a1, taken_a1, 1).wait_recv()
    narrow(wide_a1, pack_a1, taken_a1)
    exchange(pack_a1, got_a1, 3)

    for load in loads[LAT + 1 :]:
        load.wait()
    for lane in range(HALF // 128):
        longitude = (lax.broadcasted_iota(jnp.int32, (128, PEERS), 0) + 128 * lane).astype(F32)
        span = pl.ds(128 * lane, 128)
        for which in range(2):
            for parity in range(2):
                order = evens[which] if parity == 0 else (DEG - 1.0) - evens[which]
                real, imag = wave(jnp.broadcast_to(order, (128, PEERS)), longitude)
                if parity == 1:
                    real, imag = real * sign, imag * sign
                target = table_t if which == 0 else table_other
                at = 2 * PEERS * parity
                target[span, at : at + PEERS] = real.astype(BF16)
                target[span, at + PEERS : at + 2 * PEERS] = imag.astype(BF16)
    for t in range(LAT):
        latitude = lax.broadcasted_iota(jnp.int32, (NTH, PEERS), 0)
        device = lax.broadcasted_iota(jnp.int32, (NTH, PEERS), 1)
        permute[:, t * PEERS : (t + 1) * PEERS] = jnp.where(latitude == LAT * device + t, 1.0, 0.0).astype(BF16)
    rows[...] = dot(legendre[...], permute[...]).astype(BF16)
    for i in range(4):
        for j in range(LAT):
            rows_t[pl.ds(128 * j, 128), pl.ds(128 * i, 128)] = jnp.transpose(
                rows[pl.ds(128 * i, 128), pl.ds(128 * j, 128)].astype(F32)
            ).astype(BF16)
    mine = orders_s[sec, me]
    index = lax.broadcasted_iota(jnp.int32, (DEG + 1, NR), 0)
    leading = index < DEG - mine
    first = leading == (lax.rem(mine, 2) == 0)
    degree = jnp.where(leading, mine + index, index - 1).astype(F32)
    mode = lax.broadcasted_iota(jnp.int32, (1, NR), 1).astype(F32) * (1.0 / NR)
    mode4 = (mode * mode) * (mode * mode)
    mode8 = mode4 * mode4
    mode16 = mode8 * mode8
    damping = jnp.exp(-filter_strength * (mode16 * mode16 * mode4))
    factor[...] = damping / (1.0 + kappa[...] + degree * (degree + 1.0) * (1.0 / (DEG * DEG)))

    for c in range(2):
        if c == 0:
            whole(pack_a0, got_a0, 2).wait_recv()
            widen(got_a0, wide_a0)
        else:
            whole(pack_a1, got_a1, 3).wait_recv()
            widen(got_a1, wide_a1)
        for parity in range(2):
            for t in range(LAT):
                wide, span = there(c, parity, t)
                columns[t * PEERS : (t + 1) * PEERS, parity * NR : (parity + 1) * NR] = wide[span, :].astype(BF16)
        both = dot(rows[...], columns[...])
        coefficient = jnp.where(first, both[:, :NR], both[:, NR:])
        right_side = state[:, c * NR : (c + 1) * NR].astype(F32) + time_step * coefficient
        scaled = (dot(right_side.astype(BF16), right[...]) * factor[...]).astype(BF16)
        new = dot(scaled, left[...]).astype(BF16)
        new_ref[0, :, c * NR : (c + 1) * NR] = new
        new = new.astype(F32)
        split = jnp.concatenate([jnp.where(first, new, 0.0), jnp.where(first, 0.0, new)], axis=1)
        tail = split[DEG:, :]
        ends = jnp.transpose(jnp.broadcast_to(rows[DEG:, :].astype(F32), (128, NTH)))
        ends = jnp.concatenate([ends, ends], axis=1)
        sums = dot(rows_t[...], split[:DEG, :].astype(BF16)) + ends * tail
        for parity in range(2):
            for t in range(LAT):
                wide, span = back(wide_b0, wide_b1, c, parity, t)
                wide[span, :] = sums[t * PEERS : (t + 1) * PEERS, parity * NR : (parity + 1) * NR]
        if c == 0:
            narrow(wide_b0, pack_b0)
            exchange(pack_b0, got_b0, 4)
        else:
            narrow(wide_b1, pack_b1)
            for b in range(4):
                exchange(pack_b1, got_b1, 5 + b, 32 * b, min(32 * b + 32, PEERS - 1))

    whole(pack_b0, got_b0, 4).wait_recv()
    to_partner(got_b0, passed_b0, 9).start()
    widen(got_b0, wide_b0)
    y = 2 * lax.div(row, 8) + lax.div(col, 4)
    for b in range(4):
        y2 = lax.rem(y + 4 - ring(4, b), 4)
        base = 64 * lax.div(y2, 2) + 4 * lax.rem(y2, 2)
        whole(pack_b1, got_b1, 5 + b, 32 if b < 3 else 31).wait_recv()

        def pass_on(z, _):
            at = pl.multiple_of(2 * (base + 8 * z), 8)
            to_partner(got_b1.at[pl.ds(at, 8)], passed_b1.at[pl.ds(at, 8)], 10 + b).start()
            return 0

        def open_up(z, _):
            at = pl.multiple_of(2 * (base + 8 * z), 8)
            wide_b1[pl.ds(8 * at, 64), :] = got_b1[pl.ds(at, 8)].astype(F32).reshape(64, NR)
            return 0

        lax.fori_loop(0, 8, pass_on, 0)
        lax.fori_loop(0, 8, open_up, 0)

    order_sums(wide_b0, wide_b1, table_t, lambda t, value: sum_ref.__setitem__(t, value))

    to_partner(got_b0, passed_b0, 9).wait_recv()
    for b in range(4):
        to_partner(got_b1.at[pl.ds(0, 64)], passed_b1.at[pl.ds(0, 64)], 10 + b).wait_recv()
    for b in range(4):
        to_partner(got_b1.at[pl.ds(0, 64)], passed_b1.at[pl.ds(0, 64)], 10 + b).wait_send()
        whole(pack_b1, got_b1, 5 + b, 32 if b < 3 else 31).wait_send()
    to_partner(got_b0, passed_b0, 9).wait_send()
    whole(pack_b0, got_b0, 4).wait_send()
    whole(pack_a1, got_a1, 3).wait_send()
    whole(pack_a0, got_a0, 2).wait_send()
    to_partner(give_a1, taken_a1, 1).wait_send()
    to_partner(give_a0, taken_a0, 0).wait_send()


def back(wide_b0, wide_b1, c, parity, t):
    at = 12 * c + 6 * parity + t
    return (wide_b0, pl.ds(at, PEERS, stride=8)) if at < 8 else (wide_b1, pl.ds(at - 8, PEERS, stride=16))


def widen(got, wide):
    def body(i, _):
        wide[pl.ds(256 * i, 256), :] = got[pl.ds(32 * i, 32)].astype(F32).reshape(256, NR)
        return 0

    lax.fori_loop(0, got.shape[0] // 32, body, 0)


def order_sums(wide_b0, wide_b1, table, put):
    for k in range(LAT // 2):
        halves = []
        for t in (2 * k, 2 * k + 1):
            pieces = []
            for parity in range(2):
                for c in range(2):
                    wide, span = back(wide_b0, wide_b1, c, parity, t)
                    pieces.append(wide[span, :].astype(BF16))
            halves.append(jnp.concatenate(pieces, axis=0))
        sums = dot(table[...], jnp.concatenate(halves, axis=1))
        for j in range(2):
            put(2 * k + j, sums[:, j * NR : (j + 1) * NR])


def join(sum_ref, table_ref, passed_b0, passed_b1, new_ref, evolved_hbm, new_hbm, total, wide_b0, wide_b1, sem):
    copies = [pltpu.make_async_copy(new_ref, new_hbm, sem.at[LAT])]
    copies[0].start()
    widen(passed_b0, wide_b0)
    widen(passed_b1, wide_b1)

    def put(t, value):
        total[t] = sum_ref[t] + value
        copies.append(pltpu.make_async_copy(total.at[t], evolved_hbm.at[t], sem.at[t]))
        copies[-1].start()

    order_sums(wide_b0, wide_b1, table_ref, put)
    for copy in copies:
        copy.wait()


def on_device(grid_terms, pair_orders, legendre, state, kappa, right_op, left_op):
    vmem = pl.BlockSpec(memory_space=pltpu.VMEM)
    hbm = pl.BlockSpec(memory_space=pltpu.HBM)
    mib = 1024 * 1024
    grid_shape = (LAT, HALF, NR)
    spectral_shape = (1, DEG + 1, 2 * NR)

    def tiles_of(count):
        return (count * PEERS, 8, NR)

    parts = pl.pallas_call(
        kernel,
        out_shape=(
            jax.ShapeDtypeStruct(grid_shape, F32),
            jax.ShapeDtypeStruct((HALF, 4 * PEERS), BF16),
            jax.ShapeDtypeStruct(tiles_of(1), BF16),
            jax.ShapeDtypeStruct(tiles_of(2), BF16),
            jax.ShapeDtypeStruct(spectral_shape, BF16),
        ),
        in_specs=[hbm] * 7,
        out_specs=(vmem,) * 5,
        scratch_shapes=[
            pltpu.SMEM((2, PEERS), jnp.int32),
            pltpu.VMEM((2, PEERS), jnp.int32),
            pltpu.VMEM((1, NR), F32),
            pltpu.VMEM((NR, NR), BF16),
            pltpu.VMEM((NR, NR), BF16),
            pltpu.VMEM(grid_shape, F32),
            pltpu.VMEM(grid_shape, BF16),
            pltpu.VMEM((2, 4 * PEERS, HALF), BF16),
            pltpu.VMEM((HALF, 4 * PEERS), BF16),
        ]
        + [pltpu.VMEM((count * 8 * PEERS, NR), F32) for count in (2, 1, 1, 2)]
        + [pltpu.VMEM(tiles_of(count), BF16) for count in (2, 1, 1, 2, 2, 1, 1, 2, 2, 1, 2, 1)]
        + [
            pltpu.VMEM((DEG + 1, NTH), BF16),
            pltpu.VMEM((NTH, NTH), BF16),
            pltpu.VMEM((DEG + 1, NTH), BF16),
            pltpu.VMEM((NTH, DEG), BF16),
            pltpu.VMEM((DEG + 1, 2 * NR), BF16),
            pltpu.VMEM((NTH, 2 * NR), BF16),
            pltpu.VMEM((DEG + 1, NR), F32),
            pltpu.SemaphoreType.DMA((LAT + 7,)),
            pltpu.SemaphoreType.DMA((14,)),
            pltpu.SemaphoreType.DMA((14,)),
        ],
        compiler_params=pltpu.CompilerParams(collective_id=0, has_side_effects=True, vmem_limit_bytes=36 * mib),
    )(
        *(
            pltpu.with_memory_space_constraint(array, pltpu.HBM)
            for array in (
                pair_orders.reshape(2, PEERS), kappa.reshape(1, NR), right_op, left_op, grid_terms, legendre, state,
            )
        )
    )
    return pl.pallas_call(
        join,
        out_shape=(jax.ShapeDtypeStruct(grid_shape, F32), jax.ShapeDtypeStruct(spectral_shape, BF16)),
        in_specs=[vmem] * 5,
        out_specs=(hbm, hbm),
        scratch_shapes=[
            pltpu.VMEM(grid_shape, F32),
            pltpu.VMEM((8 * PEERS, NR), F32),
            pltpu.VMEM((16 * PEERS, NR), F32),
            pltpu.SemaphoreType.DMA((LAT + 1,)),
        ],
        compiler_params=pltpu.CompilerParams(vmem_limit_bytes=16 * mib),
    )(*parts)


def solution(mesh):
    return jax.shard_map(
        on_device,
        mesh=mesh,
        in_specs=(
            P(("row", "col"), "sec", None),
            P(),
            P(("sec", "row", "col"), None, None),
            P(("sec", "row", "col"), None, None),
            P(),
            P(),
            P(),
        ),
        out_specs=(P(("row", "col"), "sec", None), P(("sec", "row", "col"), None, None)),
        check_vma=False,
    )
```

time: 62.8 us -> 59.6 us (0.949)
  Pallas kernels: 62.1 us -> 58.8 us
    pallas_call x1, Pallas kernels: 60.5 us -> 56.5 us  [on_device(): pl.pallas_call(kernel, out_shape=(jax.ShapeDtypeStruct(grid_shape, F32),...]
    pallas_call x1, Pallas kernels: 1.54 us -> 2.33 us  [on_device(): pl.pallas_call(join, out_shape=(jax.ShapeDtypeStruct(grid_shape, F32), ja...]
where the time goes in v3:
time: 59.6 us; the launch traced here: 59.5 us
  Pallas kernels  58.8 us (99%)
  between operations  0.64 us (1%)
    pallas_call x1, Pallas kernels, on_device(): pl.pallas_call(kernel, out_shape=(jax.ShapeDtypeStruct(grid_shape, F32),...  56.5 us
    pallas_call x1, Pallas kernels, on_device(): pl.pallas_call(join, out_shape=(jax.ShapeDtypeStruct(grid_shape, F32), ja...  2.33 us

profile of v3, /device:TPU:1, one launch (start us, length us, event | category | flops | bytes accessed | tf_op | source)
XLA Modules:
  0.0 59.5 jit_solution(1119421908464391177)
XLA Ops:
  0.6 56.5 %shard_map.86 = (f32[6,768,128]{2,1,0:T(8,128)S(1)}, bf16[768,512]{1,0:T(8,128)(2,1)S(1)}, bf16[128,8,128]{2,1,0:T(8,128)(2,1)S(1)}, bf16[256,8,128]{2,1,0:T(8,128)(2,1)S(1)}, bf16[1,513,256]{2,1,0:T(8,128)(2,1)S(1)}) custom-call(s32[2,128]{1,0:T(2,128)} %bitcast.2, f32[1,128]{1,0:T(1,128)} %bitcast.3, bf16[128,128]{1,0:T(8,128)(2,1)} %right_hbm.1, ...), custom_call_target="tpu_custom_call" | custom-call | tf_op jit(solution)/shard_map/pallas_call | solution.py:344
  57.1 2.3 %shard_map.87 = (f32[6,768,128]{2,1,0:T(8,128)}, bf16[1,513,256]{2,1,0:T(8,128)(2,1)}) custom-call(f32[6,768,128]{2,1,0:T(8,128)S(1)} %get-tuple-element.7.sum_ref, bf16[768,512]{1,0:T(8,128)(2,1)S(1)} %get-tuple-element.8.table_ref, bf16[128,8,128]{2,1,0:T(8,128)(2,1)S(1)} %get-tuple-element.9.passed_b0, ...), custom_call_target="tpu_custom_call" | custom-call | tf_op jit(solution)/shard_map/pallas_call | solution.py:389

commit v4 on v3

--- a/solution.py
+++ b/solution.py
@@ -20,6 +20,9 @@
 PEERS = 128
 DEG = 512
 NTH = 768
+
+
+GIVE_A0, GIVE_A1, TO_A0, TO_A1, TO_B0, TO_B1, PASS_B0, PASS_B1, SEMS = 0, 4, 5, 6, 7, 8, 12, 13, 17
 
 
 def ring(count, k):
@@ -54,11 +57,11 @@
 
 def kernel(
     orders_hbm, kappa_hbm, right_hbm, left_hbm, grid_hbm, legendre_hbm, state_hbm,
-    sum_ref, table_other, passed_b0, passed_b1, new_ref,
+    sum_ref, table_other, other_b0, other_b1, new_ref,
     orders_s, orders_v, kappa, right, left,
     grid, grid_low, table, table_t,
     wide_a0, wide_a1, wide_b0, wide_b1, pack_a0, pack_a1, pack_b0, pack_b1, got_a0, got_a1, got_b0, got_b1,
-    give_a0, give_a1, taken_a0, taken_a1,
+    give_a0, give_a1, taken_a0, taken_a1, passed_b0, passed_b1,
     legendre, permute, rows, rows_t, state, columns, factor,
     load_sem, send_sem, recv_sem,
 ):
@@ -148,8 +151,38 @@
             source, target, send_sem.at[sem], recv_sem.at[sem], device_id=partner, device_id_type=MESH
         )
 
-    to_partner(give_a0, taken_a0, 0).start()
-    to_partner(give_a1, taken_a1, 1).start()
+    y = 2 * lax.div(row, 8) + lax.div(col, 4)
+
+    def run_of(y2, z):
+        return pl.multiple_of(2 * (64 * lax.div(y2, 2) + 4 * lax.rem(y2, 2) + 8 * z), 8)
+
+    def runs(body):
+        def step(z, _):
+            body(z)
+            return 0
+
+        lax.fori_loop(0, 8, step, 0)
+
+    def send_runs(source, target, y2, sem):
+        def body(z):
+            at = run_of(y2, z)
+            to_partner(source.at[pl.ds(at, 8)], target.at[pl.ds(at, 8)], sem).start()
+
+        runs(body)
+
+    def sent_runs(source, target, sem):
+        return to_partner(source.at[pl.ds(0, 64)], target.at[pl.ds(0, 64)], sem)
+
+    def widen_runs(got, wide, y2):
+        def body(z):
+            at = run_of(y2, z)
+            wide[pl.ds(8 * at, 64), :] = got[pl.ds(at, 8)].astype(F32).reshape(64, NR)
+
+        runs(body)
+
+    for b in range(4):
+        send_runs(give_a0, taken_a0, lax.rem(y + ring(4, b), 4), GIVE_A0 + b)
+    to_partner(give_a1, taken_a1, GIVE_A1).start()
 
     def exchange(pack, got, sem, start=0, stop=PEERS - 1):
         tiles = pack.shape[0] // PEERS
@@ -170,12 +203,19 @@
         count = pack.shape[0] // PEERS * messages
         return to_partner(pack.at[pl.ds(0, count)], got.at[pl.ds(0, count)], sem)
 
-    to_partner(give_a0, taken_a0, 0).wait_recv()
-    narrow(wide_a0, pack_a0, taken_a0)
-    exchange(pack_a0, got_a0, 2)
-    to_partner(give_a1, taken_a1, 1).wait_recv()
+    for b in range(4):
+        sent_runs(give_a0, taken_a0, GIVE_A0 + b).wait_recv()
+
+        def add(z):
+            at = run_of(lax.rem(y + ring(4, b), 4), z)
+            values = wide_a0[pl.ds(8 * at, 64), :].reshape(8, 8, NR) + taken_a0[pl.ds(at, 8)].astype(F32)
+            pack_a0[pl.ds(at, 8)] = values.astype(BF16)
+
+        runs(add)
+        exchange(pack_a0, got_a0, TO_A0, 32 * b, min(32 * b + 32, PEERS - 1))
+    to_partner(give_a1, taken_a1, GIVE_A1).wait_recv()
     narrow(wide_a1, pack_a1, taken_a1)
-    exchange(pack_a1, got_a1, 3)
+    exchange(pack_a1, got_a1, TO_A1)
 
     for load in loads[LAT + 1 :]:
         load.wait()
@@ -216,10 +256,10 @@
 
     for c in range(2):
         if c == 0:
-            whole(pack_a0, got_a0, 2).wait_recv()
+            whole(pack_a0, got_a0, TO_A0).wait_recv()
             widen(got_a0, wide_a0)
         else:
-            whole(pack_a1, got_a1, 3).wait_recv()
+            whole(pack_a1, got_a1, TO_A1).wait_recv()
             widen(got_a1, wide_a1)
         for parity in range(2):
             for t in range(LAT):
@@ -243,48 +283,40 @@
                 wide[span, :] = sums[t * PEERS : (t + 1) * PEERS, parity * NR : (parity + 1) * NR]
         if c == 0:
             narrow(wide_b0, pack_b0)
-            exchange(pack_b0, got_b0, 4)
+            exchange(pack_b0, got_b0, TO_B0)
         else:
             narrow(wide_b1, pack_b1)
             for b in range(4):
-                exchange(pack_b1, got_b1, 5 + b, 32 * b, min(32 * b + 32, PEERS - 1))
-
-    whole(pack_b0, got_b0, 4).wait_recv()
-    to_partner(got_b0, passed_b0, 9).start()
+                exchange(pack_b1, got_b1, TO_B1 + b, 32 * b, min(32 * b + 32, PEERS - 1))
+
+    whole(pack_b0, got_b0, TO_B0).wait_recv()
+    to_partner(got_b0, passed_b0, PASS_B0).start()
     widen(got_b0, wide_b0)
-    y = 2 * lax.div(row, 8) + lax.div(col, 4)
     for b in range(4):
         y2 = lax.rem(y + 4 - ring(4, b), 4)
-        base = 64 * lax.div(y2, 2) + 4 * lax.rem(y2, 2)
-        whole(pack_b1, got_b1, 5 + b, 32 if b < 3 else 31).wait_recv()
-
-        def pass_on(z, _):
-            at = pl.multiple_of(2 * (base + 8 * z), 8)
-            to_partner(got_b1.at[pl.ds(at, 8)], passed_b1.at[pl.ds(at, 8)], 10 + b).start()
-            return 0
-
-        def open_up(z, _):
-            at = pl.multiple_of(2 * (base + 8 * z), 8)
-            wide_b1[pl.ds(8 * at, 64), :] = got_b1[pl.ds(at, 8)].astype(F32).reshape(64, NR)
-            return 0
-
-        lax.fori_loop(0, 8, pass_on, 0)
-        lax.fori_loop(0, 8, open_up, 0)
+        whole(pack_b1, got_b1, TO_B1 + b, 32 if b < 3 else 31).wait_recv()
+        send_runs(got_b1, passed_b1, y2, PASS_B1 + b)
+        widen_runs(got_b1, wide_b1, y2)
+        if b == 0:
+            to_partner(got_b0, passed_b0, PASS_B0).wait_recv()
+            widen(passed_b0, other_b0)
+        else:
+            sent_runs(got_b1, passed_b1, PASS_B1 + b - 1).wait_recv()
+            widen_runs(passed_b1, other_b1, lax.rem(y + 4 - ring(4, b - 1), 4))
 
     order_sums(wide_b0, wide_b1, table_t, lambda t, value: sum_ref.__setitem__(t, value))
 
-    to_partner(got_b0, passed_b0, 9).wait_recv()
+    sent_runs(got_b1, passed_b1, PASS_B1 + 3).wait_recv()
+    widen_runs(passed_b1, other_b1, y)
     for b in range(4):
-        to_partner(got_b1.at[pl.ds(0, 64)], passed_b1.at[pl.ds(0, 64)], 10 + b).wait_recv()
-    for b in range(4):
-        to_partner(got_b1.at[pl.ds(0, 64)], passed_b1.at[pl.ds(0, 64)], 10 + b).wait_send()
-        whole(pack_b1, got_b1, 5 + b, 32 if b < 3 else 31).wait_send()
-    to_partner(got_b0, passed_b0, 9).wait_send()
-    whole(pack_b0, got_b0, 4).wait_send()
-    whole(pack_a1, got_a1, 3).wait_send()
-    whole(pack_a0, got_a0, 2).wait_send()
-    to_partner(give_a1, taken_a1, 1).wait_send()
-    to_partner(give_a0, taken_a0, 0).wait_send()
+        sent_runs(got_b1, passed_b1, PASS_B1 + b).wait_send()
+        whole(pack_b1, got_b1, TO_B1 + b, 32 if b < 3 else 31).wait_send()
+        sent_runs(give_a0, taken_a0, GIVE_A0 + b).wait_send()
+    to_partner(got_b0, passed_b0, PASS_B0).wait_send()
+    whole(pack_b0, got_b0, TO_B0).wait_send()
+    whole(pack_a1, got_a1, TO_A1).wait_send()
+    whole(pack_a0, got_a0, TO_A0).wait_send()
+    to_partner(give_a1, taken_a1, GIVE_A1).wait_send()
 
 
 def back(wide_b0, wide_b1, c, parity, t):
@@ -315,11 +347,9 @@
             put(2 * k + j, sums[:, j * NR : (j + 1) * NR])
 
 
-def join(sum_ref, table_ref, passed_b0, passed_b1, new_ref, evolved_hbm, new_hbm, total, wide_b0, wide_b1, sem):
+def join(sum_ref, table_ref, wide_b0, wide_b1, new_ref, evolved_hbm, new_hbm, total, sem):
     copies = [pltpu.make_async_copy(new_ref, new_hbm, sem.at[LAT])]
     copies[0].start()
-    widen(passed_b0, wide_b0)
-    widen(passed_b1, wide_b1)
 
     def put(t, value):
         total[t] = sum_ref[t] + value
@@ -346,8 +376,8 @@
         out_shape=(
             jax.ShapeDtypeStruct(grid_shape, F32),
             jax.ShapeDtypeStruct((HALF, 4 * PEERS), BF16),
-            jax.ShapeDtypeStruct(tiles_of(1), BF16),
-            jax.ShapeDtypeStruct(tiles_of(2), BF16),
+            jax.ShapeDtypeStruct((8 * PEERS, NR), F32),
+            jax.ShapeDtypeStruct((16 * PEERS, NR), F32),
             jax.ShapeDtypeStruct(spectral_shape, BF16),
         ),
         in_specs=[hbm] * 7,
@@ -364,7 +394,7 @@
             pltpu.VMEM((HALF, 4 * PEERS), BF16),
         ]
         + [pltpu.VMEM((count * 8 * PEERS, NR), F32) for count in (2, 1, 1, 2)]
-        + [pltpu.VMEM(tiles_of(count), BF16) for count in (2, 1, 1, 2, 2, 1, 1, 2, 2, 1, 2, 1)]
+        + [pltpu.VMEM(tiles_of(count), BF16) for count in (2, 1, 1, 2, 2, 1, 1, 2, 2, 1, 2, 1, 1, 2)]
         + [
             pltpu.VMEM((DEG + 1, NTH), BF16),
             pltpu.VMEM((NTH, NTH), BF16),
@@ -374,8 +404,8 @@
             pltpu.VMEM((NTH, 2 * NR), BF16),
             pltpu.VMEM((DEG + 1, NR), F32),
             pltpu.SemaphoreType.DMA((LAT + 7,)),
-            pltpu.SemaphoreType.DMA((14,)),
-            pltpu.SemaphoreType.DMA((14,)),
+            pltpu.SemaphoreType.DMA((SEMS,)),
+            pltpu.SemaphoreType.DMA((SEMS,)),
         ],
         compiler_params=pltpu.CompilerParams(collective_id=0, has_side_effects=True, vmem_limit_bytes=36 * mib),
     )(
@@ -393,8 +423,6 @@
         out_specs=(hbm, hbm),
         scratch_shapes=[
             pltpu.VMEM(grid_shape, F32),
-            pltpu.VMEM((8 * PEERS, NR), F32),
-            pltpu.VMEM((16 * PEERS, NR), F32),
             pltpu.SemaphoreType.DMA((LAT + 1,)),
         ],
         compiler_params=pltpu.CompilerParams(vmem_limit_bytes=16 * mib),

time: 59.6 us -> 58.9 us (0.988)
  Pallas kernels: 58.8 us -> 58.2 us
where the time goes in v4:
time: 58.9 us; the launch traced here: 58.8 us
  Pallas kernels  58.2 us (99%)
  between operations  0.64 us (1%)
    pallas_call x1, Pallas kernels, on_device(): pl.pallas_call(kernel, out_shape=(jax.ShapeDtypeStruct(grid_shape, F32),...  56 us
    pallas_call x1, Pallas kernels, on_device(): pl.pallas_call(join, out_shape=(jax.ShapeDtypeStruct(grid_shape, F32), ja...  2.19 us

profile of v4, /device:TPU:1, one launch (start us, length us, event | category | flops | bytes accessed | tf_op | source)
XLA Modules:
  0.0 58.8 jit_solution(16794525007567237598)
XLA Ops:
  0.6 56.0 %shard_map.86 = (f32[6,768,128]{2,1,0:T(8,128)S(1)}, bf16[768,512]{1,0:T(8,128)(2,1)S(1)}, f32[1024,128]{1,0:T(8,128)S(1)}, f32[2048,128]{1,0:T(8,128)S(1)}, bf16[1,513,256]{2,1,0:T(8,128)(2,1)S(1)}) custom-call(s32[2,128]{1,0:T(2,128)} %bitcast.2, f32[1,128]{1,0:T(1,128)} %bitcast.3, bf16[128,128]{1,0:T(8,128)(2,1)} %right_hbm.1, ...), custom_call_target="tpu_custom_call" | custom-call | tf_op jit(solution)/shard_map/pallas_call | solution.py:374
  56.6 2.2 %shard_map.87 = (f32[6,768,128]{2,1,0:T(8,128)}, bf16[1,513,256]{2,1,0:T(8,128)(2,1)}) custom-call(f32[6,768,128]{2,1,0:T(8,128)S(1)} %get-tuple-element.7.sum_ref, bf16[768,512]{1,0:T(8,128)(2,1)S(1)} %get-tuple-element.8.table_ref, f32[1024,128]{1,0:T(8,128)S(1)} %get-tuple-element.9.wide_b0, f32[2048,128]{1,0:T(8,128)S(1)} %get-tuple-element.10.wide_b1, ...), custom_call_target="tpu_custom_call" | custom-call | tf_op jit(solution)/shard_map/pallas_call | solution.py:419

commit v5 on v4

--- a/solution.py
+++ b/solution.py
@@ -26,15 +26,27 @@
 
 
 def ring(count, k):
-    return count // 2 + lax.div(k + 1, 2) * (1 - 2 * lax.rem(k, 2))
-
-
-def peer_of(i, row, col):
+    return count // 2 + (k + 1) // 2 * (1 - 2 * (k % 2))
+
+
+def each_peer(row, col, body, first=0, last=16):
     z, y, x = lax.rem(row, 8), 2 * lax.div(row, 8) + lax.div(col, 4), lax.rem(col, 4)
-    z2 = lax.rem(z + ring(8, lax.rem(i, 8)), 8)
-    x2 = lax.rem(x + ring(4, lax.rem(lax.div(i, 8), 4)), 4)
-    y2 = lax.rem(y + ring(4, lax.div(i, 32)), 4)
-    return 8 * lax.div(y2, 2) + z2, 4 * lax.rem(y2, 2) + x2
+    along = [lax.rem(z + ring(8, k), 8) for k in range(8)]
+
+    def line(i, count):
+        x2 = lax.rem(x + ring(4, lax.rem(i, 4)), 4)
+        y2 = lax.rem(y + ring(4, lax.div(i, 4)), 4)
+        row2, col2 = 8 * lax.div(y2, 2), 4 * lax.rem(y2, 2) + x2
+        for z2 in along[:count]:
+            body(row2 + z2, col2)
+
+    def step(i, _):
+        line(i, 8)
+        return 0
+
+    lax.fori_loop(first, min(last, 15), step, 0)
+    if last == 16:
+        line(jnp.int32(15), 7)
 
 
 def wave(order, longitude):
@@ -82,13 +94,11 @@
 
     barrier = pltpu.get_barrier_semaphore()
 
-    def greet(i, _):
-        row2, col2 = peer_of(i, row, col)
+    def greet(row2, col2):
         pl.semaphore_signal(barrier, inc=1, device_id=(sec, row2, col2), device_id_type=MESH)
-        return 0
 
     pl.semaphore_signal(barrier, inc=1, device_id=partner, device_id_type=MESH)
-    lax.fori_loop(0, PEERS - 1, greet, 0)
+    each_peer(row, col, greet)
 
     loads[0].wait()
     evens = []
@@ -184,19 +194,17 @@
         send_runs(give_a0, taken_a0, lax.rem(y + ring(4, b), 4), GIVE_A0 + b)
     to_partner(give_a1, taken_a1, GIVE_A1).start()
 
-    def exchange(pack, got, sem, start=0, stop=PEERS - 1):
+    def exchange(pack, got, sem, first=0, last=16):
         tiles = pack.shape[0] // PEERS
 
-        def body(i, _):
-            row2, col2 = peer_of(i, row, col)
+        def send(row2, col2):
             pltpu.make_async_remote_copy(
                 pack.at[pl.ds(tiles * (8 * row2 + col2), tiles)], got.at[pl.ds(tiles * me, tiles)],
                 send_sem.at[sem], recv_sem.at[sem], device_id=(sec, row2, col2), device_id_type=MESH,
             ).start()
-            return 0
-
-        lax.fori_loop(start, stop, body, 0)
-        if stop == PEERS - 1:
+
+        each_peer(row, col, send, first, last)
+        if last == 16:
             got[pl.ds(tiles * me, tiles)] = pack[pl.ds(tiles * me, tiles)]
 
     def whole(pack, got, sem, messages=PEERS - 1):
@@ -212,7 +220,7 @@
             pack_a0[pl.ds(at, 8)] = values.astype(BF16)
 
         runs(add)
-        exchange(pack_a0, got_a0, TO_A0, 32 * b, min(32 * b + 32, PEERS - 1))
+        exchange(pack_a0, got_a0, TO_A0, 4 * b, 4 * b + 4)
     to_partner(give_a1, taken_a1, GIVE_A1).wait_recv()
     narrow(wide_a1, pack_a1, taken_a1)
     exchange(pack_a1, got_a1, TO_A1)
@@ -287,7 +295,7 @@
         else:
             narrow(wide_b1, pack_b1)
             for b in range(4):
-                exchange(pack_b1, got_b1, TO_B1 + b, 32 * b, min(32 * b + 32, PEERS - 1))
+                exchange(pack_b1, got_b1, TO_B1 + b, 4 * b, 4 * b + 4)
 
     whole(pack_b0, got_b0, TO_B0).wait_recv()
     to_partner(got_b0, passed_b0, PASS_B0).start()

time: 58.9 us -> 56.9 us (0.966)
  Pallas kernels: 58.2 us -> 56.2 us
    pallas_call x1, Pallas kernels: 56 us -> 54 us  [on_device(): pl.pallas_call(kernel, out_shape=(jax.ShapeDtypeStruct(grid_shape, F32),...]
where the time goes in v5:
time: 56.9 us
  Pallas kernels  56.2 us (99%)
  between operations  0.64 us (1%)
    pallas_call x1, Pallas kernels, on_device(): pl.pallas_call(kernel, out_shape=(jax.ShapeDtypeStruct(grid_shape, F32),...  54 us
    pallas_call x1, Pallas kernels, on_device(): pl.pallas_call(join, out_shape=(jax.ShapeDtypeStruct(grid_shape, F32), ja...  2.19 us

profile of v5, /device:TPU:1, one launch (start us, length us, event | category | flops | bytes accessed | tf_op | source)
XLA Modules:
  0.0 56.9 jit_solution(3549351123966768658)
XLA Ops:
  0.6 54.0 %shard_map.86 = (f32[6,768,128]{2,1,0:T(8,128)S(1)}, bf16[768,512]{1,0:T(8,128)(2,1)S(1)}, f32[1024,128]{1,0:T(8,128)S(1)}, f32[2048,128]{1,0:T(8,128)S(1)}, bf16[1,513,256]{2,1,0:T(8,128)(2,1)S(1)}) custom-call(s32[2,128]{1,0:T(2,128)} %bitcast.2, f32[1,128]{1,0:T(1,128)} %bitcast.3, bf16[128,128]{1,0:T(8,128)(2,1)} %right_hbm.1, ...), custom_call_target="tpu_custom_call" | custom-call | tf_op jit(solution)/shard_map/pallas_call | solution.py:382
  54.7 2.2 %shard_map.87 = (f32[6,768,128]{2,1,0:T(8,128)}, bf16[1,513,256]{2,1,0:T(8,128)(2,1)}) custom-call(f32[6,768,128]{2,1,0:T(8,128)S(1)} %get-tuple-element.7.sum_ref, bf16[768,512]{1,0:T(8,128)(2,1)S(1)} %get-tuple-element.8.table_ref, f32[1024,128]{1,0:T(8,128)S(1)} %get-tuple-element.9.wide_b0, f32[2048,128]{1,0:T(8,128)S(1)} %get-tuple-element.10.wide_b1, ...), custom_call_target="tpu_custom_call" | custom-call | tf_op jit(solution)/shard_map/pallas_call | solution.py:427

commit v6 on v5

--- a/solution.py
+++ b/solution.py
@@ -74,7 +74,7 @@
     grid, grid_low, table, table_t,
     wide_a0, wide_a1, wide_b0, wide_b1, pack_a0, pack_a1, pack_b0, pack_b1, got_a0, got_a1, got_b0, got_b1,
     give_a0, give_a1, taken_a0, taken_a1, passed_b0, passed_b1,
-    legendre, permute, rows, rows_t, state, columns, factor,
+    legendre, permute, rows, rows_t, state, columns, factor, ends, chosen,
     load_sem, send_sem, recv_sem,
 ):
     sec, row, col = lax.axis_index("sec"), lax.axis_index("row"), lax.axis_index("col")
@@ -237,9 +237,9 @@
                 if parity == 1:
                     real, imag = real * sign, imag * sign
                 target = table_t if which == 0 else table_other
-                at = 2 * PEERS * parity
+                at = PEERS * parity
                 target[span, at : at + PEERS] = real.astype(BF16)
-                target[span, at + PEERS : at + 2 * PEERS] = imag.astype(BF16)
+                target[span, at + 2 * PEERS : at + 3 * PEERS] = imag.astype(BF16)
     for t in range(LAT):
         latitude = lax.broadcasted_iota(jnp.int32, (NTH, PEERS), 0)
         device = lax.broadcasted_iota(jnp.int32, (NTH, PEERS), 1)
@@ -250,10 +250,11 @@
             rows_t[pl.ds(128 * j, 128), pl.ds(128 * i, 128)] = jnp.transpose(
                 rows[pl.ds(128 * i, 128), pl.ds(128 * j, 128)].astype(F32)
             ).astype(BF16)
+    ends[...] = jnp.transpose(jnp.broadcast_to(rows[DEG:, :].astype(F32), (128, NTH)))
     mine = orders_s[sec, me]
     index = lax.broadcasted_iota(jnp.int32, (DEG + 1, NR), 0)
     leading = index < DEG - mine
-    first = leading == (lax.rem(mine, 2) == 0)
+    chosen[...] = jnp.where(leading == (lax.rem(mine, 2) == 0), 1.0, 0.0)
     degree = jnp.where(leading, mine + index, index - 1).astype(F32)
     mode = lax.broadcasted_iota(jnp.int32, (1, NR), 1).astype(F32) * (1.0 / NR)
     mode4 = (mode * mode) * (mode * mode)
@@ -269,6 +270,7 @@
         else:
             whole(pack_a1, got_a1, TO_A1).wait_recv()
             widen(got_a1, wide_a1)
+        first = chosen[...] > 0.5
         for parity in range(2):
             for t in range(LAT):
                 wide, span = there(c, parity, t)
@@ -282,24 +284,39 @@
         new = new.astype(F32)
         split = jnp.concatenate([jnp.where(first, new, 0.0), jnp.where(first, 0.0, new)], axis=1)
         tail = split[DEG:, :]
-        ends = jnp.transpose(jnp.broadcast_to(rows[DEG:, :].astype(F32), (128, NTH)))
-        ends = jnp.concatenate([ends, ends], axis=1)
-        sums = dot(rows_t[...], split[:DEG, :].astype(BF16)) + ends * tail
-        for parity in range(2):
-            for t in range(LAT):
+        split = split[:DEG, :].astype(BF16)
+        for t in range(LAT):
+            block = slice(t * PEERS, (t + 1) * PEERS)
+            sums = dot(rows_t[block, :], split)
+            for parity in range(2):
                 wide, span = back(wide_b0, wide_b1, c, parity, t)
-                wide[span, :] = sums[t * PEERS : (t + 1) * PEERS, parity * NR : (parity + 1) * NR]
+                half = slice(parity * NR, (parity + 1) * NR)
+                wide[span, :] = sums[:, half] + ends[block, :] * tail[:, half]
         if c == 0:
             narrow(wide_b0, pack_b0)
             exchange(pack_b0, got_b0, TO_B0)
         else:
-            narrow(wide_b1, pack_b1)
             for b in range(4):
+
+                def cut(z):
+                    at = run_of(lax.rem(y + ring(4, b), 4), z)
+                    pack_b1[pl.ds(at, 8)] = wide_b1[pl.ds(8 * at, 64), :].reshape(8, 8, NR).astype(BF16)
+
+                runs(cut)
                 exchange(pack_b1, got_b1, TO_B1 + b, 4 * b, 4 * b + 4)
 
     whole(pack_b0, got_b0, TO_B0).wait_recv()
     to_partner(got_b0, passed_b0, PASS_B0).start()
     widen(got_b0, wide_b0)
+
+    def put_sum(t, value):
+        sum_ref[t] = value
+
+    def add_sum(t, value):
+        sum_ref[t] = sum_ref[t] + value
+
+    for k in range(2):
+        order_sums(wide_b0, wide_b1, table_t, k, (0,), put_sum)
     for b in range(4):
         y2 = lax.rem(y + 4 - ring(4, b), 4)
         whole(pack_b1, got_b1, TO_B1 + b, 32 if b < 3 else 31).wait_recv()
@@ -308,11 +325,15 @@
         if b == 0:
             to_partner(got_b0, passed_b0, PASS_B0).wait_recv()
             widen(passed_b0, other_b0)
+            for k in range(2):
+                order_sums(other_b0, other_b1, table_other, k, (0,), add_sum)
         else:
             sent_runs(got_b1, passed_b1, PASS_B1 + b - 1).wait_recv()
             widen_runs(passed_b1, other_b1, lax.rem(y + 4 - ring(4, b - 1), 4))
 
-    order_sums(wide_b0, wide_b1, table_t, lambda t, value: sum_ref.__setitem__(t, value))
+    for k in range(2):
+        order_sums(wide_b0, wide_b1, table_t, k, (1,), add_sum)
+    order_sums(wide_b0, wide_b1, table_t, 2, (0, 1), put_sum)
 
     sent_runs(got_b1, passed_b1, PASS_B1 + 3).wait_recv()
     widen_runs(passed_b1, other_b1, y)
@@ -328,8 +349,10 @@
 
 
 def back(wide_b0, wide_b1, c, parity, t):
-    at = 12 * c + 6 * parity + t
-    return (wide_b0, pl.ds(at, PEERS, stride=8)) if at < 8 else (wide_b1, pl.ds(at - 8, PEERS, stride=16))
+    if c == 0 and t < 4:
+        return wide_b0, pl.ds(4 * parity + t, PEERS, stride=8)
+    at = 12 * c - 8 + 6 * parity + t if c == 1 else 2 * parity + t - 4
+    return wide_b1, pl.ds(at, PEERS, stride=16)
 
 
 def widen(got, wide):
@@ -340,19 +363,19 @@
     lax.fori_loop(0, got.shape[0] // 32, body, 0)
 
 
-def order_sums(wide_b0, wide_b1, table, put):
-    for k in range(LAT // 2):
-        halves = []
-        for t in (2 * k, 2 * k + 1):
-            pieces = []
+def order_sums(wide_b0, wide_b1, table, k, parts, put):
+    halves = []
+    for t in (2 * k, 2 * k + 1):
+        pieces = []
+        for c in parts:
             for parity in range(2):
-                for c in range(2):
-                    wide, span = back(wide_b0, wide_b1, c, parity, t)
-                    pieces.append(wide[span, :].astype(BF16))
-            halves.append(jnp.concatenate(pieces, axis=0))
-        sums = dot(table[...], jnp.concatenate(halves, axis=1))
-        for j in range(2):
-            put(2 * k + j, sums[:, j * NR : (j + 1) * NR])
+                wide, span = back(wide_b0, wide_b1, c, parity, t)
+                pieces.append(wide[span, :].astype(BF16))
+        halves.append(jnp.concatenate(pieces, axis=0))
+    columns = slice(2 * PEERS * parts[0], 2 * PEERS * (parts[-1] + 1))
+    sums = dot(table[:, columns], jnp.concatenate(halves, axis=1))
+    for j in range(2):
+        put(2 * k + j, sums[:, j * NR : (j + 1) * NR])
 
 
 def join(sum_ref, table_ref, wide_b0, wide_b1, new_ref, evolved_hbm, new_hbm, total, sem):
@@ -364,7 +387,9 @@
         copies.append(pltpu.make_async_copy(total.at[t], evolved_hbm.at[t], sem.at[t]))
         copies[-1].start()
 
-    order_sums(wide_b0, wide_b1, table_ref, put)
+    for k in range(2):
+        order_sums(wide_b0, wide_b1, table_ref, k, (1,), put)
+    order_sums(wide_b0, wide_b1, table_ref, 2, (0, 1), put)
     for copy in copies:
         copy.wait()
 
@@ -411,6 +436,8 @@
             pltpu.VMEM((DEG + 1, 2 * NR), BF16),
             pltpu.VMEM((NTH, 2 * NR), BF16),
             pltpu.VMEM((DEG + 1, NR), F32),
+            pltpu.VMEM((NTH, NR), F32),
+            pltpu.VMEM((DEG + 1, NR), F32),
             pltpu.SemaphoreType.DMA((LAT + 7,)),
             pltpu.SemaphoreType.DMA((SEMS,)),
             pltpu.SemaphoreType.DMA((SEMS,)),

time: 56.9 us -> 56.7 us (level)
  no operation moved by 1% of the time
where the time goes in v6:
time: 56.7 us; the launch traced here: 56.6 us
  Pallas kernels  55.9 us (99%)
  between operations  0.64 us (1%)
    pallas_call x1, Pallas kernels, on_device(): pl.pallas_call(kernel, out_shape=(jax.ShapeDtypeStruct(grid_shape, F32),...  53.9 us
    pallas_call x1, Pallas kernels, on_device(): pl.pallas_call(join, out_shape=(jax.ShapeDtypeStruct(grid_shape, F32), ja...  2.01 us

profile of v6, /device:TPU:1, one launch (start us, length us, event | category | flops | bytes accessed | tf_op | source)
XLA Modules:
  0.0 56.6 jit_solution(5992242919072596788)
XLA Ops:
  0.6 53.9 %shard_map.86 = (f32[6,768,128]{2,1,0:T(8,128)S(1)}, bf16[768,512]{1,0:T(8,128)(2,1)S(1)}, f32[1024,128]{1,0:T(8,128)S(1)}, f32[2048,128]{1,0:T(8,128)S(1)}, bf16[1,513,256]{2,1,0:T(8,128)(2,1)S(1)}) custom-call(s32[2,128]{1,0:T(2,128)} %bitcast.2, f32[1,128]{1,0:T(1,128)} %bitcast.3, bf16[128,128]{1,0:T(8,128)(2,1)} %right_hbm.1, ...), custom_call_target="tpu_custom_call" | custom-call | tf_op jit(solution)/shard_map/pallas_call | solution.py:407
  54.6 2.0 %shard_map.87 = (f32[6,768,128]{2,1,0:T(8,128)}, bf16[1,513,256]{2,1,0:T(8,128)(2,1)}) custom-call(f32[6,768,128]{2,1,0:T(8,128)S(1)} %get-tuple-element.7.sum_ref, bf16[768,512]{1,0:T(8,128)(2,1)S(1)} %get-tuple-element.8.table_ref, f32[1024,128]{1,0:T(8,128)S(1)} %get-tuple-element.9.wide_b0, f32[2048,128]{1,0:T(8,128)S(1)} %get-tuple-element.10.wide_b1, ...), custom_call_target="tpu_custom_call" | custom-call | tf_op jit(solution)/shard_map/pallas_call | solution.py:454
